TPU v7x, 32 devices: a whole 2x2x4 slice. The times are simulated.
32 devices in a mesh: space: 2 (over y), chan: 4 (over x, core), rep: 4 (over z).
Axes of the slice: x: 2, y: 2, z: 4, core: 2. Of those that a mesh axis runs over, the one named last changes fastest.
Arguments:
- volume: bfloat16 [4, 192, 2, 1024], P('rep', 'chan', 'space'), may hold values from -6 to 6
- weights: bfloat16 [27, 192, 192], replicated, may hold values from -0.078125 to 0.078125
- grad_out: bfloat16 [4, 192, 2, 1024], P('rep', 'chan', 'space'), may hold values from -6 to 6
Outputs:
- conv_out: bfloat16 [4, 192, 2, 1024], P('rep', 'chan', 'space')
- grad_in: bfloat16 [4, 192, 2, 1024], P('rep', 'chan', 'space')
- grad_weights: bfloat16 [27, 192, 192], P(None, None, 'chan')
All inputs are finite; a program needn't handle non-finite values.
Results may differ from a plain program's by a relative error of at most 0.0014.
Values may be sent and summed in bfloat16 or wider, within the bound.
No kernel may reach another device: no remote copies, remote signals or barrier semaphores. Data moves between devices by JAX's collectives and lax.ppermute only.
A program may use at most 64 MiB of HBM per device.

v0:
```python
import functools
import math

import jax
import jax.numpy as jnp
from jax import lax
from jax.experimental import pallas as pl
from jax.experimental.pallas import tpu as pltpu
from jax.sharding import PartitionSpec as P


H = 32
W = 32

OFFSETS = (-1, 0, 1)
LANES = 128
SUBLANES = 8
KERNEL_VMEM = 16 << 20


def extended(x, sides, width):
    for axis, dim in sides:
        peers, length = (lax.axis_size(axis), x.shape[dim])
        up = [(i, (i + 1) % peers) for i in range(peers)]
        down = [(j, i) for i, j in up]
        last = lax.slice_in_dim(x, length - width, length, axis=dim)
        first = lax.slice_in_dim(x, 0, width, axis=dim)
        before = lax.ppermute(last, axis, up)
        after = lax.ppermute(first, axis, down)
        x = jnp.concatenate([before, x, after], axis=dim)
    return x


def tap_number(depth_off, row_off, col_off):
    return (depth_off + 1) * 9 + (row_off + 1) * 3 + (col_off + 1)


def moved_block(padded, depth_off, row_off, col_off):
    samples, channels, depth_pad, rows_pad, width = padded.shape
    depth = depth_pad - 2
    rows = rows_pad - 2
    piece = padded[:, :, 1 + depth_off : 1 + depth_off + depth, 1 + row_off : 1 + row_off + rows, :]
    piece = jnp.roll(piece, -col_off, axis=4)
    return piece.reshape(samples, channels, depth * rows * width)


def spatial_layer(volume, weights, grad_out):
    samples, chan_block, depth, cells = volume.shape
    channels = weights.shape[1]
    vol_grid = volume.reshape(samples, chan_block, depth, H, W)
    grad_grid = grad_out.reshape(samples, chan_block, depth, H, W)
    row_volume, row_grad = (
        lax.all_to_all(vol_grid, "chan", split_axis=3, concat_axis=1, tiled=True),
        lax.all_to_all(grad_grid, "chan", split_axis=3, concat_axis=1, tiled=True),
    )
    rows = row_volume.shape[3]
    padded_vol = extended(row_volume, (("space", 2), ("chan", 3)), 1)
    padded_grad = extended(row_grad, (("space", 2), ("chan", 3)), 1)
    interior = moved_block(padded_vol, 0, 0, 0)
    conv_sum = jnp.zeros((samples, channels, depth * rows * W), jnp.float32)
    back_sum = jnp.zeros((samples, channels, depth * rows * W), jnp.float32)
    kernel_rows = []
    for depth_off in OFFSETS:
        for row_off in OFFSETS:
            for col_off in OFFSETS:
                tap = tap_number(depth_off, row_off, col_off)
                moved_in = moved_block(padded_vol, depth_off, row_off, col_off)
                conv_sum = conv_sum + jnp.einsum(
                    "ic,bip->bcp", weights[tap], moved_in, preferred_element_type=jnp.float32
                )
                moved_grad = moved_block(padded_grad, -depth_off, -row_off, -col_off)
                back_sum = back_sum + jnp.einsum(
                    "ic,bcp->bip", weights[tap], moved_grad, preferred_element_type=jnp.float32
                )
                kernel_rows.append(
                    jnp.einsum(
                        "bip,bcp->ic", interior, moved_grad, preferred_element_type=jnp.float32
                    )
                )
    conv_rows = conv_sum.astype(jnp.bfloat16).reshape(samples, channels, depth, rows, W)
    back_rows = back_sum.astype(jnp.bfloat16).reshape(samples, channels, depth, rows, W)
    conv_back, grad_back = (
        lax.all_to_all(conv_rows, "chan", split_axis=1, concat_axis=3, tiled=True),
        lax.all_to_all(back_rows, "chan", split_axis=1, concat_axis=3, tiled=True),
    )
    conv_out = conv_back.reshape(samples, chan_block, depth, cells)
    grad_in = grad_back.reshape(samples, chan_block, depth, cells)
    kernel_full = jnp.stack(kernel_rows)
    kernel_part = lax.psum_scatter(kernel_full, "chan", scatter_dimension=2, tiled=True)
    factor = 1.0 / math.sqrt(
        samples * lax.axis_size("rep") * depth * lax.axis_size("space") * cells
    )
    grad_weights = (lax.psum(kernel_part, ("space", "rep")) * factor).astype(jnp.bfloat16)
    return (conv_out, grad_in, grad_weights)


def power_of_two(n):
    return n > 0 and n & (n - 1) == 0


def whole_sample_fits(volume, weights):
    samples, chan_block, depth, cells = volume.shape
    peers = lax.axis_size("chan")
    return (
        (samples, depth, lax.axis_size("space")) == (1, 1, 2)
        and power_of_two(peers)
        and peers > 1
        and power_of_two(lax.axis_size("rep"))
        and chan_block % 16 == 0
        and weights.shape[1] == chan_block * peers
        and LANES < weights.shape[1] < 2 * LANES
        and 2 * (weights.shape[1] - LANES) == LANES
        and LANES % W == 0
        and cells == H * W
    )


def xor_pairs(n, k):
    return [(i, i ^ k) for i in range(n)]


def even_offsets(peers):
    return range(0, peers, 2)


def from_peer(x, space_off, chan_off):
    peers = lax.axis_size("chan")
    if not space_off:
        return lax.ppermute(x, "chan", xor_pairs(peers, chan_off))
    if not chan_off:
        return lax.ppermute(x, "space", xor_pairs(2, 1))
    pairs = xor_pairs(2 * peers, peers ^ chan_off)
    return lax.ppermute(x, ("space", "chan"), pairs)


def gathered(x):
    blocks = {(0, 0): x}
    for space_off in (0, 1):
        for chan_off in even_offsets(lax.axis_size("chan")):
            if space_off or chan_off:
                blocks[space_off, chan_off] = from_peer(x, space_off, chan_off)
    for (space_off, chan_off), block in list(blocks.items()):
        blocks[space_off, chan_off ^ 1] = from_peer(block, 0, 1)
    return blocks


def gathered_pairs(pair):
    pairs = {0: pair}
    for chan_off in range(1, lax.axis_size("chan")):
        pairs[chan_off] = from_peer(pair, 0, chan_off)
    return pairs


def moved_cols(x, step):
    if not step:
        return x
    pieces = []
    for at in range(0, x.shape[1], LANES):
        piece = x[:, at : at + LANES]
        lane = lax.broadcasted_iota(jnp.int32, piece.shape, 1) % W
        edge = W - 1 if step > 0 else 0
        near = pltpu.roll(piece, (-step) % LANES, 1)
        far = pltpu.roll(piece, (step * (W - 1)) % LANES, 1)
        pieces.append(jnp.where(lane == edge, far, near))
    return jnp.concatenate(pieces, axis=1)


def moved_rows(x, step):
    if not step:
        return x
    return pltpu.roll(x, (-step * W) % x.shape[1], 1)


def put_block(plane_ref, chan_off, block):
    size = block.shape[0]
    at = pl.multiple_of((lax.axis_index("chan") ^ chan_off) * size, size)
    plane_ref[pl.ds(at, size), :] = block


def prepare_body(weight_ref, forward_ref, backward_ref, held, sems):
    channels = weight_ref.shape[1]
    taps = len(OFFSETS) ** 2
    size = backward_ref.shape[1]
    copies = []
    for depth in range(len(OFFSETS)):
        part = pl.ds(depth * taps, taps)
        copies.append(pltpu.make_async_copy(weight_ref.at[part], held.at[part], sems.at[depth]))
    at = pl.multiple_of(lax.axis_index("chan") * size, size)
    rows_copy = pltpu.make_async_copy(
        weight_ref.at[:, pl.ds(at, size), :], backward_ref, sems.at[len(OFFSETS)]
    )
    for copy in copies:
        copy.start()
    rows_copy.start()
    row = lax.broadcasted_iota(jnp.int32, (size, channels), 0)
    column = lax.broadcasted_iota(jnp.int32, (size, channels), 1)
    chosen = (column == row + lax.axis_index("chan") * size).astype(jnp.bfloat16)
    for depth, copy in enumerate(copies):
        copy.wait()
        for at in range(taps):
            rows = lax.dot_general(
                chosen,
                held[depth * taps + at],
                (((1,), (1,)), ((), ())),
                preferred_element_type=jnp.float32,
            )
            forward_ref[depth, at * size : (at + 1) * size, :] = rows.astype(jnp.bfloat16)
    rows_copy.wait()


def kernel_grad_body(keys, rep, chunk, *refs):
    block_refs, (own_ref, other_ref), refs = refs[: len(keys)], refs[len(keys) : len(keys) + 2], refs[len(keys) + 2 :]
    out_refs, planes, (pair_ref, moved, packed) = refs[:rep], refs[rep : rep + 2], refs[rep + 2 :]
    for ref, (space_off, chan_off) in zip(block_refs, keys, strict=True):
        put_block(planes[space_off], chan_off, ref[...])
    block, size = own_ref.shape[0], own_ref.shape[0] // 2
    pair_ref[:block, :] = own_ref[...]
    pair_ref[block:, :] = other_ref[...]
    first = lax.axis_index("space") == 0
    half = moved.shape[0] // 2
    for source, start in ((own_ref, 0), (other_ref, half)):
        source = source[...].astype(jnp.float32)
        source = jnp.where(first, source[:size], source[size:])
        for col_off in OFFSETS:
            cols = moved_cols(source, -col_off)
            for row_off in OFFSETS:
                at = start + ((row_off + 1) * 3 + col_off + 1) * size
                moved[pl.ds(at, size), :] = moved_rows(cols, -row_off).astype(jnp.bfloat16)
    contract = (((1,), (1,)), ((), ()))
    with_own, with_other = (
        lax.dot_general(moved[...], plane[...], contract, preferred_element_type=jnp.float32)
        for plane in planes
    )
    total = with_own + jnp.concatenate([with_other[half:], with_other[:half]], axis=0)
    taps = total.shape[0]
    packed[pl.ds(0, taps), :] = total[:, :LANES]
    rest = total[:, LANES:]
    packed[pl.ds(taps, taps // 2), :] = jnp.concatenate([rest[: taps // 2], rest[taps // 2 :]], axis=1)
    used = taps + taps // 2
    if packed.shape[0] > used:
        packed[pl.ds(used, packed.shape[0] - used), :] = jnp.zeros(
            (packed.shape[0] - used, LANES), jnp.float32
        )
    mine = lax.axis_index("rep")
    for k, out_ref in enumerate(out_refs):
        at = pl.multiple_of((mine ^ k) * chunk, SUBLANES)
        out_ref[...] = packed[pl.ds(at, chunk), :]


def total_body(factor, *refs):
    *part_refs, out_ref = refs
    total = part_refs[0][...]
    for ref in part_refs[1:]:
        total = total + ref[...]
    out_ref[...] = (total * factor).astype(out_ref.dtype)


def convolve(sign, weights_of, own_plane, other_plane, out_ref):
    size = out_ref.shape[0]

    def product(depth_off, plane):
        return jnp.dot(weights_of(depth_off), plane[...], preferred_element_type=jnp.float32)

    total = product(0, own_plane) + product(-1, other_plane) + product(1, other_plane)
    out = None
    for col_off in OFFSETS:
        rows = None
        for row_off in OFFSETS:
            at = ((row_off + 1) * 3 + col_off + 1) * size
            piece = moved_rows(total[at : at + size], sign * row_off)
            rows = piece if rows is None else rows + piece
        rows = moved_cols(rows, sign * col_off)
        out = rows if out is None else out + rows
    out_ref[...] = out.astype(out_ref.dtype)


def forward_body(own_plane, other_plane, weight_ref, out_ref):
    convolve(1, lambda depth_off: weight_ref[depth_off + 1], own_plane, other_plane, out_ref)


def backward_body(keys, *refs):
    pair_refs = refs[: len(keys)]
    weight_ref, out_ref, own_plane, other_plane = refs[len(keys) :]
    size, channels = out_ref.shape[0], weight_ref.shape[2]
    taps = len(OFFSETS) ** 2
    for ref, chan_off in zip(pair_refs, keys, strict=True):
        put_block(own_plane, chan_off, ref[:size, :])
        put_block(other_plane, chan_off, ref[size:, :])

    def weights_of(depth_off):
        rows = weight_ref[(depth_off + 1) * taps : (depth_off + 2) * taps]
        return rows.reshape(taps * size, channels)

    convolve(-1, weights_of, own_plane, other_plane, out_ref)


def merge_body(*refs):
    *part_refs, out_ref = refs
    size = part_refs[0].shape[0]
    for i, ref in enumerate(part_refs):
        out_ref[i * size : (i + 1) * size, :] = ref[...]


def assemble_body(chunk, near_ref, near_other_ref, far_ref, far_other_ref, out_ref, packed):
    space, mine = lax.axis_index("space"), lax.axis_index("rep")
    for y, refs in ((space, (near_ref, far_ref)), (space ^ 1, (near_other_ref, far_other_ref))):
        k = 0
        for ref in refs:
            for start in range(0, ref.shape[0], chunk):
                at = pl.multiple_of((mine ^ k) * chunk, SUBLANES)
                packed[y, pl.ds(at, chunk), :] = ref[start : start + chunk, :].astype(jnp.float32)
                k += 1
    size = out_ref.shape[1] // 2
    around = len(OFFSETS) ** 2
    half = size * around
    for depth_off in OFFSETS:
        held = abs(depth_off)
        for i in range(around):
            tap = (depth_off + 1) * around + i
            for y in (0, 1):
                rows = slice(y * size, (y + 1) * size)
                at = held * half + i * size
                out_ref[tap, rows, :LANES] = packed[y, at : at + size, :].astype(out_ref.dtype)
                at = 2 * half + i * size
                lanes = slice(held * LANES // 2, (held + 1) * LANES // 2)
                out_ref[tap, rows, LANES:] = packed[y, at : at + size, lanes].astype(out_ref.dtype)


def call(body, out_shape, scratch, flops, *operands, in_place=0):
    in_vmem = pl.BlockSpec(memory_space=pltpu.VMEM)
    spaces = [pltpu.HBM] * in_place + [pltpu.VMEM] * (len(operands) - in_place)
    operands = [
        pltpu.with_memory_space_constraint(x, space)
        for x, space in zip(operands, spaces, strict=True)
    ]
    return pl.pallas_call(
        body,
        out_shape=out_shape,
        in_specs=[pl.BlockSpec(memory_space=space) for space in spaces],
        out_specs=jax.tree.map(lambda _: in_vmem, out_shape),
        scratch_shapes=scratch,
        compiler_params=pltpu.CompilerParams(vmem_limit_bytes=KERNEL_VMEM),
        cost_estimate=pl.CostEstimate(
            flops=flops,
            transcendentals=0,
            bytes_accessed=sum(x.size * x.dtype.itemsize for x in operands),
        ),
    )(*operands)


def whole_sample_layer(volume, weights, grad_out):
    samples, chan_block, depth, cells = volume.shape
    channels = weights.shape[1]
    rep, space = lax.axis_size("rep"), lax.axis_size("space")
    vol = volume.reshape(chan_block, cells)
    grad = grad_out.reshape(chan_block, cells)

    vol_blocks = gathered(vol)
    keys = sorted(vol_blocks)
    grad_other = from_peer(grad, 1, 0)

    around = len(OFFSETS) ** 2
    taps = around * chan_block
    used = taps * channels // LANES
    chunk = -(-used // (rep * SUBLANES)) * SUBLANES
    plane = pltpu.VMEM((channels, cells), jnp.bfloat16)
    flops = 2 * 2 * taps * channels * cells
    forward_weights, backward_weights = call(
        prepare_body,
        [
            pltpu.VMEM((len(OFFSETS), taps, channels), jnp.bfloat16),
            pltpu.VMEM((weights.shape[0], chan_block, channels), jnp.bfloat16),
        ],
        [
            pltpu.VMEM(weights.shape, jnp.bfloat16),
            pltpu.SemaphoreType.DMA((len(OFFSETS) + 1,)),
        ],
        2 * weights.size * chan_block,
        weights,
        in_place=1,
    )
    *parts, own_plane, other_plane, pair = call(
        functools.partial(kernel_grad_body, keys, rep, chunk),
        [pltpu.VMEM((chunk, LANES), jnp.float32)] * rep
        + [plane, plane, pltpu.VMEM((2 * chan_block, cells), jnp.bfloat16)],
        [pltpu.VMEM((taps, cells), jnp.bfloat16), pltpu.VMEM((chunk * rep, LANES), jnp.float32)],
        flops,
        *[vol_blocks[k] for k in keys],
        grad,
        grad_other,
    )
    received = [parts[0]]
    for k in range(1, rep):
        received.append(lax.ppermute(parts[k], "rep", xor_pairs(rep, k)))
    factor = 1.0 / math.sqrt(samples * rep * depth * space * cells)
    kernel_sum = call(
        functools.partial(total_body, factor),
        pltpu.VMEM((chunk, LANES), jnp.bfloat16),
        [],
        rep * chunk * LANES,
        *received,
    )

    grad_pairs = gathered_pairs(pair)
    pair_keys = sorted(grad_pairs)
    out_type = jax.ShapeDtypeStruct((chan_block, cells), jnp.bfloat16)
    conv_out = call(
        forward_body, out_type, [], 3 * flops // 2, own_plane, other_plane, forward_weights
    )
    grad_in = call(
        functools.partial(backward_body, pair_keys),
        out_type,
        [plane, plane],
        3 * flops // 2,
        *[grad_pairs[k] for k in pair_keys],
        backward_weights,
    )

    spread = [kernel_sum]
    for k in range(1, rep):
        spread.append(lax.ppermute(kernel_sum, "rep", xor_pairs(rep, k)))
    across = []
    for held in (spread[:2], spread[2:]):
        merged_type = pltpu.VMEM((len(held) * chunk, LANES), jnp.bfloat16)
        merged = call(merge_body, merged_type, [], 0, *held)
        across += [merged, lax.ppermute(merged, "space", xor_pairs(2, 1))]
    grad_weights = call(
        functools.partial(assemble_body, chunk),
        jax.ShapeDtypeStruct((weights.shape[0], chan_block, channels), jnp.bfloat16),
        [pltpu.VMEM((space, chunk * rep, LANES), jnp.float32)],
        0,
        *across,
    )
    return (
        conv_out.reshape(volume.shape),
        grad_in.reshape(volume.shape),
        jnp.swapaxes(grad_weights, 1, 2),
    )


def on_device(volume, weights, grad_out):
    if whole_sample_fits(volume, weights):
        return whole_sample_layer(volume, weights, grad_out)
    return spatial_layer(volume, weights, grad_out)


def solution(mesh):
    return jax.shard_map(
        on_device,
        mesh=mesh,
        in_specs=(P("rep", "chan", "space", None), P(), P("rep", "chan", "space", None)),
        out_specs=(
            P("rep", "chan", "space", None),
            P("rep", "chan", "space", None),
            P(None, None, "chan"),
        ),
        check_vma=False,
    )
```

profile of v0, /device:TPU:0, one launch (start us, length us, event | category | flops | bytes accessed | tf_op | source)
XLA Modules:
  0.0 43.0 jit_solution(15084715365790364588)
XLA Ops:
  0.6 3.0 %collective-permute-start.1 = (bf16[48,1024]{1,0:T(8,128)(2,1)}, bf16[48,1024]{1,0:T(8,128)(2,1)S(1)}, u32[]{:S(2)}, u32[]{:S(2)}) collective-permute-start(bf16[48,1024]{1,0:T(8,128)(2,1)} %bitcast.5), channel_id=1, source_target_pairs={{0,8},{4,12},{8,0},{12,4},{1,9},{5,13},{9,1},{13,5},{2,10},{6,14},... | collective-permute-start | bytes 294920 | tf_op jit(solution)/shard_map/ppermute | solution.py:129
  3.7 1.5 %collective-permute-start.3 = (bf16[48,1024]{1,0:T(8,128)(2,1)}, bf16[48,1024]{1,0:T(8,128)(2,1)S(1)}, u32[]{:S(2)}, u32[]{:S(2)}) collective-permute-start(bf16[48,1024]{1,0:T(8,128)(2,1)} %bitcast.6), channel_id=1, source_target_pairs={{0,16},{16,0},{1,17},{17,1},{2,18},{18,2},{3,19},{19,3},{4,20},{20... | collective-permute-start | bytes 294920 | tf_op jit(solution)/shard_map/ppermute | solution.py:131
  5.2 0.0 collective-permute-start.5
  5.2 0.0 collective-permute-start
  5.2 2.0 %collective-permute-start.7 = (bf16[48,1024]{1,0:T(8,128)(2,1)}, bf16[48,1024]{1,0:T(8,128)(2,1)S(1)}, u32[]{:S(2)}, u32[]{:S(2)}) collective-permute-start(bf16[48,1024]{1,0:T(8,128)(2,1)} %bitcast.10), channel_id=1, source_target_pairs={{0,16},{16,0},{1,17},{17,1},{2,18},{18,2},{3,19},{19,3},{4,20},{20... | collective-permute-start | bytes 294920 | tf_op jit(solution)/shard_map/ppermute | solution.py:131
  7.2 0.0 collective-permute-done.1.refs_2_
  7.2 0.2 collective-permute-start.2
  7.4 2.4 %collective-permute-done.3.refs_4_ = bf16[48,1024]{1,0:T(8,128)(2,1)S(1)} collective-permute-done((bf16[48,1024]{1,0:T(8,128)(2,1)}, bf16[48,1024]{1,0:T(8,128)(2,1)S(1)}, u32[]{:S(2)}, u32[]{:S(2)}) %collective-permute-start.3) | collective-permute-done | bytes 98336 | tf_op jit(solution)/shard_map/ppermute | solution.py:131
  9.8 0.0 collective-permute-start.4
  9.8 1.2 %collective-permute-done.5.refs_6_ = bf16[48,1024]{1,0:T(8,128)(2,1)S(1)} collective-permute-done((bf16[48,1024]{1,0:T(8,128)(2,1)}, bf16[48,1024]{1,0:T(8,128)(2,1)S(1)}, u32[]{:S(2)}, u32[]{:S(2)}) %collective-permute-start.5) | collective-permute-done | bytes 98336 | tf_op jit(solution)/shard_map/ppermute | solution.py:133
  11.0 1.7 %collective-permute-done.7.refs_9_ = bf16[48,1024]{1,0:T(8,128)(2,1)S(1)} collective-permute-done((bf16[48,1024]{1,0:T(8,128)(2,1)}, bf16[48,1024]{1,0:T(8,128)(2,1)S(1)}, u32[]{:S(2)}, u32[]{:S(2)}) %collective-permute-start.7) | collective-permute-done | bytes 98336 | tf_op jit(solution)/shard_map/ppermute | solution.py:131
  12.7 0.0 collective-permute-done.2.refs_3_
  12.7 0.0 collective-permute-done.4.refs_5_
  12.7 0.9 %copy-done = bf16[1,48,1,1024]{3,1,2,0:T(8,128)(2,1)S(1)} copy-done((bf16[1,48,1,1024]{3,1,2,0:T(8,128)(2,1)S(1)}, bf16[1,48,1,1024]{3,1,2,0:T(8,128)(2,1)}, u32[]{:S(2)}) %copy-start) | copy-done | bytes 98328
  13.6 0.9 %copy-done.1 = bf16[1,48,1,1024]{3,1,2,0:T(8,128)(2,1)S(1)} copy-done((bf16[1,48,1,1024]{3,1,2,0:T(8,128)(2,1)S(1)}, bf16[1,48,1,1024]{3,1,2,0:T(8,128)(2,1)}, u32[]{:S(2)}) %copy-start.1) | copy-done | bytes 98328
  14.5 1.1 %shard_map.58 = (f32[168,128]{1,0:T(8,128)S(1)}, f32[168,128]{1,0:T(8,128)S(1)}, f32[168,128]{1,0:T(8,128)S(1)}, f32[168,128]{1,0:T(8,128)S(1)}, bf16[192,1024]{...) custom-call(bf16[48,1024]{1,0:T(8,128)(2,1)S(1)} %bitcast.9, ...), custom_call_target="tpu_custom_call" | custom-call | flops 339738624 | bytes 983040 | tf_op jit(solution)/shard_map/pallas_call | solution.py:336
  15.6 1.6 %collective-permute-start.11 = (f32[168,128]{1,0:T(8,128)S(1)}, f32[168,128]{1,0:T(8,128)S(1)}, u32[]{:S(2)}, u32[]{:S(2)}) collective-permute-start(f32[168,128]{1,0:T(8,128)S(1)} %get-tuple-element.18), channel_id=1, source_target_pairs={{0,1},{1,0},{2,3},{3,2},{4,5},{5,4},{6,7},{7,6},{8,9},{9,8},{10,11... | collective-permute-start | bytes 258056 | tf_op jit(solution)/shard_map/ppermute | solution.py:394
  17.2 2.6 %collective-permute-start.12 = (f32[168,128]{1,0:T(8,128)S(1)}, f32[168,128]{1,0:T(8,128)S(1)}, u32[]{:S(2)}, u32[]{:S(2)}) collective-permute-start(f32[168,128]{1,0:T(8,128)S(1)} %get-tuple-element.19), channel_id=1, source_target_pairs={{0,2},{1,3},{2,0},{3,1},{4,6},{5,7},{6,4},{7,5},{8,10},{9,11},{10,... | collective-permute-start | bytes 258056 | tf_op jit(solution)/shard_map/ppermute | solution.py:394
  19.8 0.2 collective-permute-start.13
  20.0 1.0 %collective-permute-start.9 = (bf16[96,1024]{1,0:T(8,128)(2,1)S(1)}, bf16[96,1024]{1,0:T(8,128)(2,1)S(1)}, u32[]{:S(2)}, u32[]{:S(2)}) collective-permute-start(bf16[96,1024]{1,0:T(8,128)(2,1)S(1)} %get-tuple-element.15.refs_0_), channel_id=1, source_target_pairs={{0,8},{4,12},{8,0},{12,4},{1,9},{5,13},{9,1},{13,5},{2,10},{6,14},... | collective-permute-start | bytes 589832 | tf_op jit(solution)/shard_map/ppermute | solution.py:129
  21.0 0.9 %collective-permute-start.10 = (bf16[96,1024]{1,0:T(8,128)(2,1)S(1)}, bf16[96,1024]{1,0:T(8,128)(2,1)S(1)}, u32[]{:S(2)}, u32[]{:S(2)}) collective-permute-start(bf16[96,1024]{1,0:T(8,128)(2,1)S(1)} %get-tuple-element.15.refs_0_), channel_id=1, source_target_pairs={{0,12},{4,8},{8,4},{12,0},{1,13},{5,9},{9,5},{13,1},{2,14},{6,10},... | collective-permute-start | bytes 589832 | tf_op jit(solution)/shard_map/ppermute | solution.py:129
  21.9 4.9 %collective-permute-done.12.refs_2_ = f32[168,128]{1,0:T(8,128)S(1)} collective-permute-done((f32[168,128]{1,0:T(8,128)S(1)}, f32[168,128]{1,0:T(8,128)S(1)}, u32[]{:S(2)}, u32[]{:S(2)}) %collective-permute-start.12) | collective-permute-done | bytes 86048 | tf_op jit(solution)/shard_map/ppermute | solution.py:394
  26.8 1.5 %collective-permute-start.14 = (bf16[168,128]{1,0:T(8,128)(2,1)S(1)}, bf16[168,128]{1,0:T(8,128)(2,1)S(1)}, u32[]{:S(2)}, u32[]{:S(2)}) collective-permute-start(bf16[168,128]{1,0:T(8,128)(2,1)S(1)} %shard_map.62.refs_0_), channel_id=1, source_target_pairs={{0,1},{1,0},{2,3},{3,2},{4,5},{5,4},{6,7},{7,6},{8,9},{9,8},{10,11... | collective-permute-start | bytes 129032 | tf_op jit(solution)/shard_map/ppermute | solution.py:421
  28.4 1.5 %collective-permute-start.16 = (bf16[168,128]{1,0:T(8,128)(2,1)S(1)}, bf16[168,128]{1,0:T(8,128)(2,1)S(1)}, u32[]{:S(2)}, u32[]{:S(2)}) collective-permute-start(bf16[168,128]{1,0:T(8,128)(2,1)S(1)} %shard_map.62.refs_0_), channel_id=1, source_target_pairs={{0,2},{1,3},{2,0},{3,1},{4,6},{5,7},{6,4},{7,5},{8,10},{9,11},{10,... | collective-permute-start | bytes 129032 | tf_op jit(solution)/shard_map/ppermute | solution.py:421
  29.9 1.2 %collective-permute-done.14.refs_1_ = bf16[168,128]{1,0:T(8,128)(2,1)S(1)} collective-permute-done((bf16[168,128]{1,0:T(8,128)(2,1)S(1)}, bf16[168,128]{1,0:T(8,128)(2,1)S(1)}, u32[]{:S(2)}, u32[]{:S(2)}) %collective-permute-start.14) | collective-permute-done | bytes 43040 | tf_op jit(solution)/shard_map/ppermute | solution.py:421
  31.1 2.3 %collective-permute-start.17 = (bf16[168,128]{1,0:T(8,128)(2,1)S(1)}, bf16[168,128]{1,0:T(8,128)(2,1)S(1)}, u32[]{:S(2)}, u32[]{:S(2)}) collective-permute-start(bf16[168,128]{1,0:T(8,128)(2,1)S(1)} %shard_map.62.refs_0_), channel_id=1, source_target_pairs={{0,3},{1,2},{2,1},{3,0},{4,7},{5,6},{6,5},{7,4},{8,11},{9,10},{10,... | collective-permute-start | bytes 129032 | tf_op jit(solution)/shard_map/ppermute | solution.py:421
  33.4 2.5 %shard_map.59 = (bf16[3,432,192]{2,1,0:T(8,128)(2,1)S(1)}, bf16[27,48,192]{2,1,0:T(8,128)(2,1)S(1)}) custom-call(bf16[27,192,192]{2,1,0:T(8,128)(2,1)} %weight_ref.1), custom_call_target="tpu_custom_call" | custom-call | flops 95551488 | bytes 1990656 | tf_op jit(solution)/shard_map/pallas_call | solution.py:336
  35.9 1.4 %collective-permute-start.15 = (bf16[336,128]{1,0:T(8,128)(2,1)S(1)}, bf16[336,128]{1,0:T(8,128)(2,1)S(1)}, u32[]{:S(2)}, u32[]{:S(2)}) collective-permute-start(bf16[336,128]{1,0:T(8,128)(2,1)S(1)} %shard_map.63.near_ref), channel_id=1, source_target_pairs={{0,16},{16,0},{1,17},{17,1},{2,18},{18,2},{3,19},{19,3},{4,20},{20... | collective-permute-start | bytes 258056 | tf_op jit(solution)/shard_map/ppermute | solution.py:426
  37.3 0.8 %collective-permute-start.18 = (bf16[336,128]{1,0:T(8,128)(2,1)S(1)}, bf16[336,128]{1,0:T(8,128)(2,1)S(1)}, u32[]{:S(2)}, u32[]{:S(2)}) collective-permute-start(bf16[336,128]{1,0:T(8,128)(2,1)S(1)} %shard_map.64.far_ref), channel_id=1, source_target_pairs={{0,16},{16,0},{1,17},{17,1},{2,18},{18,2},{3,19},{19,3},{4,20},{20... | collective-permute-start | bytes 258056 | tf_op jit(solution)/shard_map/ppermute | solution.py:426
  38.2 1.8 %shard_map.60 = bf16[48,1024]{1,0:T(8,128)(2,1)} custom-call(bf16[192,1024]{1,0:T(8,128)(2,1)S(1)} %get-tuple-element.12.own_plane, bf16[192,1024]{1,0:T(8,128)(2,1)S(1)} %get-tuple-element.13.other_plane, bf16[3,432,192]{2,1,0:T(8,128)(2,1)S(1)} %get-tuple-element.14.weight_ref), custom_call_target="tpu_custom_call" | custom-call | flops 509607936 | bytes 1284096 | tf_op jit(solution)/shard_map/pallas_call | solution.py:336
  40.0 1.9 %shard_map.61 = bf16[48,1024]{1,0:T(8,128)(2,1)} custom-call(bf16[96,1024]{1,0:T(8,128)(2,1)S(1)} %get-tuple-element.15.refs_0_, bf16[96,1024]{1,0:T(8,128)(2,1)S(1)} %collective-permute-done.8.refs_1_, bf16[96,1024]{1,0:T(8,128)(2,1)S(1)} %collective-permute-done.9.refs_2_, bf16[96,1024]{1,0:T(8,128)(2,1)S(1)} %collective-permute-done.10.refs_3_, ...), custom_call_target="tpu_custom_call" | custom-call | flops 509607936 | bytes 1284096 | tf_op jit(solution)/shard_map/pallas_call | solution.py:336
  41.9 1.1 %shard_map.65 = bf16[27,48,192]{2,1,0:T(8,128)(2,1)} custom-call(bf16[336,128]{1,0:T(8,128)(2,1)S(1)} %shard_map.63.near_ref, bf16[336,128]{1,0:T(8,128)(2,1)S(1)} %collective-permute-done.15.near_other_ref, bf16[336,128]{1,0:T(8,128)(2,1)S(1)} %shard_map.64.far_ref, bf16[336,128]{1,0:T(8,128)(2,1)S(1)} %collective-permute-done.18.far_other_ref), custom_call_target="tpu_custom_call" | custom-call | bytes 344064 | tf_op jit(solution)/shard_map/pallas_call | solution.py:336
  (18 shorter events, 0.1 us)
Async XLA Ops:
  0.6 6.6 %collective-permute-start.1 = (bf16[48,1024]{1,0:T(8,128)(2,1)}, bf16[48,1024]{1,0:T(8,128)(2,1)S(1)}, u32[]{:S(2)}, u32[]{:S(2)}) collective-permute-start(bf16[48,1024]{1,0:T(8,128)(2,1)} %bitcast.5), channel_id=1, source_target_pairs={{0,8},{4,12},{8,0},{12,4},{1,9},{5,13},{9,1},{13,5},{2,10},{6,14},... | collective-permute-start | bytes 294920 | tf_op jit(solution)/shard_map/ppermute | solution.py:129
  3.7 6.1 %collective-permute-start.3 = (bf16[48,1024]{1,0:T(8,128)(2,1)}, bf16[48,1024]{1,0:T(8,128)(2,1)S(1)}, u32[]{:S(2)}, u32[]{:S(2)}) collective-permute-start(bf16[48,1024]{1,0:T(8,128)(2,1)} %bitcast.6), channel_id=1, source_target_pairs={{0,16},{16,0},{1,17},{17,1},{2,18},{18,2},{3,19},{19,3},{4,20},{20... | collective-permute-start | bytes 294920 | tf_op jit(solution)/shard_map/ppermute | solution.py:131
  5.2 5.8 %collective-permute-start.5 = (bf16[48,1024]{1,0:T(8,128)(2,1)}, bf16[48,1024]{1,0:T(8,128)(2,1)S(1)}, u32[]{:S(2)}, u32[]{:S(2)}) collective-permute-start(bf16[48,1024]{1,0:T(8,128)(2,1)} %bitcast.7), channel_id=1, source_target_pairs={{0,24},{4,28},{8,16},{12,20},{16,8},{20,12},{24,0},{28,4},{1,25},{... | collective-permute-start | bytes 294920 | tf_op jit(solution)/shard_map/ppermute | solution.py:133
  5.2 5.8 %collective-permute-start = (bf16[48,1024]{1,0:T(8,128)(2,1)}, bf16[48,1024]{1,0:T(8,128)(2,1)S(1)}, u32[]{:S(2)}, u32[]{:S(2)}) collective-permute-start(bf16[48,1024]{1,0:T(8,128)(2,1)} %bitcast.8), channel_id=1, source_target_pairs={{0,4},{4,0},{8,12},{12,8},{1,5},{5,1},{9,13},{13,9},{2,6},{6,2},{1... | collective-permute-start | bytes 294920 | tf_op jit(solution)/shard_map/ppermute | solution.py:129
  5.2 7.5 %collective-permute-start.7 = (bf16[48,1024]{1,0:T(8,128)(2,1)}, bf16[48,1024]{1,0:T(8,128)(2,1)S(1)}, u32[]{:S(2)}, u32[]{:S(2)}) collective-permute-start(bf16[48,1024]{1,0:T(8,128)(2,1)} %bitcast.10), channel_id=1, source_target_pairs={{0,16},{16,0},{1,17},{17,1},{2,18},{18,2},{3,19},{19,3},{4,20},{20... | collective-permute-start | bytes 294920 | tf_op jit(solution)/shard_map/ppermute | solution.py:131
  7.2 5.5 %collective-permute-start.2 = (bf16[48,1024]{1,0:T(8,128)(2,1)S(1)}, bf16[48,1024]{1,0:T(8,128)(2,1)S(1)}, u32[]{:S(2)}, u32[]{:S(2)}) collective-permute-start(bf16[48,1024]{1,0:T(8,128)(2,1)S(1)} %collective-permute-done.1.refs_2_), channel_id=1, source_target_pairs={{0,4},{4,0},{8,12},{12,8},{1,5},{5,1},{9,13},{13,9},{2,6},{6,2},{1... | collective-permute-start | bytes 294920 | tf_op jit(solution)/shard_map/ppermute | solution.py:129
  9.8 2.9 %collective-permute-start.4 = (bf16[48,1024]{1,0:T(8,128)(2,1)S(1)}, bf16[48,1024]{1,0:T(8,128)(2,1)S(1)}, u32[]{:S(2)}, u32[]{:S(2)}) collective-permute-start(bf16[48,1024]{1,0:T(8,128)(2,1)S(1)} %collective-permute-done.3.refs_4_), channel_id=1, source_target_pairs={{0,4},{4,0},{8,12},{12,8},{1,5},{5,1},{9,13},{13,9},{2,6},{6,2},{1... | collective-permute-start | bytes 294920 | tf_op jit(solution)/shard_map/ppermute | solution.py:129
  11.0 1.7 %collective-permute-start.6 = (bf16[48,1024]{1,0:T(8,128)(2,1)S(1)}, bf16[48,1024]{1,0:T(8,128)(2,1)S(1)}, u32[]{:S(2)}, u32[]{:S(2)}) collective-permute-start(bf16[48,1024]{1,0:T(8,128)(2,1)S(1)} %collective-permute-done.5.refs_6_), channel_id=1, source_target_pairs={{0,4},{4,0},{8,12},{12,8},{1,5},{5,1},{9,13},{13,9},{2,6},{6,2},{1... | collective-permute-start | bytes 294920 | tf_op jit(solution)/shard_map/ppermute | solution.py:129
  12.7 0.9 %copy-start = (bf16[1,48,1,1024]{3,1,2,0:T(8,128)(2,1)S(1)}, bf16[1,48,1,1024]{3,1,2,0:T(8,128)(2,1)}, u32[]{:S(2)}) copy-start(bf16[1,48,1,1024]{3,1,2,0:T(8,128)(2,1)} %param.3) | copy-start | bytes 294916
  13.6 0.9 %copy-start.1 = (bf16[1,48,1,1024]{3,1,2,0:T(8,128)(2,1)S(1)}, bf16[1,48,1,1024]{3,1,2,0:T(8,128)(2,1)}, u32[]{:S(2)}) copy-start(bf16[1,48,1,1024]{3,1,2,0:T(8,128)(2,1)} %param.5) | copy-start | bytes 294916
  15.6 5.4 %collective-permute-start.11 = (f32[168,128]{1,0:T(8,128)S(1)}, f32[168,128]{1,0:T(8,128)S(1)}, u32[]{:S(2)}, u32[]{:S(2)}) collective-permute-start(f32[168,128]{1,0:T(8,128)S(1)} %get-tuple-element.18), channel_id=1, source_target_pairs={{0,1},{1,0},{2,3},{3,2},{4,5},{5,4},{6,7},{7,6},{8,9},{9,8},{10,11... | collective-permute-start | bytes 258056 | tf_op jit(solution)/shard_map/ppermute | solution.py:394
  17.2 9.6 %collective-permute-start.12 = (f32[168,128]{1,0:T(8,128)S(1)}, f32[168,128]{1,0:T(8,128)S(1)}, u32[]{:S(2)}, u32[]{:S(2)}) collective-permute-start(f32[168,128]{1,0:T(8,128)S(1)} %get-tuple-element.19), channel_id=1, source_target_pairs={{0,2},{1,3},{2,0},{3,1},{4,6},{5,7},{6,4},{7,5},{8,10},{9,11},{10,... | collective-permute-start | bytes 258056 | tf_op jit(solution)/shard_map/ppermute | solution.py:394
  19.8 7.0 %collective-permute-start.13 = (f32[168,128]{1,0:T(8,128)S(1)}, f32[168,128]{1,0:T(8,128)S(1)}, u32[]{:S(2)}, u32[]{:S(2)}) collective-permute-start(f32[168,128]{1,0:T(8,128)S(1)} %get-tuple-element.20), channel_id=1, source_target_pairs={{0,3},{1,2},{2,1},{3,0},{4,7},{5,6},{6,5},{7,4},{8,11},{9,10},{10,... | collective-permute-start | bytes 258056 | tf_op jit(solution)/shard_map/ppermute | solution.py:394
  20.0 20.0 %collective-permute-start.8 = (bf16[96,1024]{1,0:T(8,128)(2,1)S(1)}, bf16[96,1024]{1,0:T(8,128)(2,1)S(1)}, u32[]{:S(2)}, u32[]{:S(2)}) collective-permute-start(bf16[96,1024]{1,0:T(8,128)(2,1)S(1)} %get-tuple-element.15.refs_0_), channel_id=1, source_target_pairs={{0,4},{4,0},{8,12},{12,8},{1,5},{5,1},{9,13},{13,9},{2,6},{6,2},{1... | collective-permute-start | bytes 589832 | tf_op jit(solution)/shard_map/ppermute | solution.py:129
  20.0 20.0 %collective-permute-start.9 = (bf16[96,1024]{1,0:T(8,128)(2,1)S(1)}, bf16[96,1024]{1,0:T(8,128)(2,1)S(1)}, u32[]{:S(2)}, u32[]{:S(2)}) collective-permute-start(bf16[96,1024]{1,0:T(8,128)(2,1)S(1)} %get-tuple-element.15.refs_0_), channel_id=1, source_target_pairs={{0,8},{4,12},{8,0},{12,4},{1,9},{5,13},{9,1},{13,5},{2,10},{6,14},... | collective-permute-start | bytes 589832 | tf_op jit(solution)/shard_map/ppermute | solution.py:129
  21.0 19.0 %collective-permute-start.10 = (bf16[96,1024]{1,0:T(8,128)(2,1)S(1)}, bf16[96,1024]{1,0:T(8,128)(2,1)S(1)}, u32[]{:S(2)}, u32[]{:S(2)}) collective-permute-start(bf16[96,1024]{1,0:T(8,128)(2,1)S(1)} %get-tuple-element.15.refs_0_), channel_id=1, source_target_pairs={{0,12},{4,8},{8,4},{12,0},{1,13},{5,9},{9,5},{13,1},{2,14},{6,10},... | collective-permute-start | bytes 589832 | tf_op jit(solution)/shard_map/ppermute | solution.py:129
  26.8 4.3 %collective-permute-start.14 = (bf16[168,128]{1,0:T(8,128)(2,1)S(1)}, bf16[168,128]{1,0:T(8,128)(2,1)S(1)}, u32[]{:S(2)}, u32[]{:S(2)}) collective-permute-start(bf16[168,128]{1,0:T(8,128)(2,1)S(1)} %shard_map.62.refs_0_), channel_id=1, source_target_pairs={{0,1},{1,0},{2,3},{3,2},{4,5},{5,4},{6,7},{7,6},{8,9},{9,8},{10,11... | collective-permute-start | bytes 129032 | tf_op jit(solution)/shard_map/ppermute | solution.py:421
  28.4 7.5 %collective-permute-start.16 = (bf16[168,128]{1,0:T(8,128)(2,1)S(1)}, bf16[168,128]{1,0:T(8,128)(2,1)S(1)}, u32[]{:S(2)}, u32[]{:S(2)}) collective-permute-start(bf16[168,128]{1,0:T(8,128)(2,1)S(1)} %shard_map.62.refs_0_), channel_id=1, source_target_pairs={{0,2},{1,3},{2,0},{3,1},{4,6},{5,7},{6,4},{7,5},{8,10},{9,11},{10,... | collective-permute-start | bytes 129032 | tf_op jit(solution)/shard_map/ppermute | solution.py:421
  31.1 6.2 %collective-permute-start.17 = (bf16[168,128]{1,0:T(8,128)(2,1)S(1)}, bf16[168,128]{1,0:T(8,128)(2,1)S(1)}, u32[]{:S(2)}, u32[]{:S(2)}) collective-permute-start(bf16[168,128]{1,0:T(8,128)(2,1)S(1)} %shard_map.62.refs_0_), channel_id=1, source_target_pairs={{0,3},{1,2},{2,1},{3,0},{4,7},{5,6},{6,5},{7,4},{8,11},{9,10},{10,... | collective-permute-start | bytes 129032 | tf_op jit(solution)/shard_map/ppermute | solution.py:421
  35.9 6.0 %collective-permute-start.15 = (bf16[336,128]{1,0:T(8,128)(2,1)S(1)}, bf16[336,128]{1,0:T(8,128)(2,1)S(1)}, u32[]{:S(2)}, u32[]{:S(2)}) collective-permute-start(bf16[336,128]{1,0:T(8,128)(2,1)S(1)} %shard_map.63.near_ref), channel_id=1, source_target_pairs={{0,16},{16,0},{1,17},{17,1},{2,18},{18,2},{3,19},{19,3},{4,20},{20... | collective-permute-start | bytes 258056 | tf_op jit(solution)/shard_map/ppermute | solution.py:426
  37.3 4.6 %collective-permute-start.18 = (bf16[336,128]{1,0:T(8,128)(2,1)S(1)}, bf16[336,128]{1,0:T(8,128)(2,1)S(1)}, u32[]{:S(2)}, u32[]{:S(2)}) collective-permute-start(bf16[336,128]{1,0:T(8,128)(2,1)S(1)} %shard_map.64.far_ref), channel_id=1, source_target_pairs={{0,16},{16,0},{1,17},{17,1},{2,18},{18,2},{3,19},{19,3},{4,20},{20... | collective-permute-start | bytes 258056 | tf_op jit(solution)/shard_map/ppermute | solution.py:426
where the time goes:
time: 43.2 us; the launch traced here: 43 us
  starting transfers between devices  20.7 us (48%)
  waiting for transfers between devices  11.4 us (26%)
  Pallas kernels  8.39 us (19%)
  local copies, waits for them, and re-layouts  1.78 us (4%)
  between operations  0.7 us (2%)
    pallas_call x8, Pallas kernels, call(): pl.pallas_call(body, out_shape=out_shape, in_specs=[pl.BlockSpec(memory_s...  8.39 us
    ppermute x3, starting transfers between devices, whole_sample_layer(): spread.append(lax.ppermute(kernel_sum, 'rep', xor_pairs(rep, k)))  5.37 us
    ppermute x8, starting transfers between devices, from_peer(): return lax.ppermute(x, 'chan', xor_pairs(peers, chan_off))  5.13 us
    ppermute x3, waiting for transfers between devices, whole_sample_layer(): received.append(lax.ppermute(parts[k], 'rep', xor_pairs(rep, k)))  4.9 us
    ppermute x3, starting transfers between devices, whole_sample_layer(): received.append(lax.ppermute(parts[k], 'rep', xor_pairs(rep, k)))  4.45 us
    ppermute x2, waiting for transfers between devices, from_peer(): return lax.ppermute(x, 'space', xor_pairs(2, 1))  4.05 us
    ppermute x2, starting transfers between devices, from_peer(): return lax.ppermute(x, 'space', xor_pairs(2, 1))  3.5 us
    ppermute x2, starting transfers between devices, whole_sample_layer(): across += [merged, lax.ppermute(merged, 'space', xor_pairs(2, 1))]  2.25 us
  transfers between devices with their start and end apart: 19, of which 5 were waited for; matrix products, arithmetic and copies ran while one was open for 0% of the time, Pallas kernels for 15%

commit v1 on v0

--- a/solution.py
+++ b/solution.py
@@ -208,19 +208,36 @@
     rows_copy.wait()
 
 
+def held_body(grad_ref, vol_ref, mine_ref, sent_ref, held_ref, sems):
+    half = mine_ref.shape[0]
+    copies = [pltpu.make_async_copy(vol_ref, held_ref, sems.at[2])]
+    for i, ref in enumerate((mine_ref, sent_ref)):
+        at = pl.multiple_of((lax.axis_index("space") ^ i) * half, SUBLANES)
+        copies.append(pltpu.make_async_copy(grad_ref.at[pl.ds(at, half)], ref, sems.at[i]))
+    for copy in copies:
+        copy.start()
+    for copy in copies:
+        copy.wait()
+
+
+def pair_body(mine_ref, sent_ref, other_mine_ref, other_rest_ref, pair_ref):
+    first = lax.axis_index("space") == 0
+    size = pair_ref.shape[0] // 2
+    for i, refs in enumerate(((mine_ref, sent_ref), (other_mine_ref, other_rest_ref))):
+        mine, rest = (ref[...].astype(jnp.float32) for ref in refs)
+        whole = jnp.concatenate([jnp.where(first, mine, rest), jnp.where(first, rest, mine)], axis=0)
+        pair_ref[i * size : (i + 1) * size, :] = whole.astype(pair_ref.dtype)
+
+
 def kernel_grad_body(keys, rep, chunk, *refs):
     block_refs, (own_ref, other_ref), refs = refs[: len(keys)], refs[len(keys) : len(keys) + 2], refs[len(keys) + 2 :]
-    out_refs, planes, (pair_ref, moved, packed) = refs[:rep], refs[rep : rep + 2], refs[rep + 2 :]
+    out_refs, planes, (moved, packed) = refs[:rep], refs[rep : rep + 2], refs[rep + 2 :]
     for ref, (space_off, chan_off) in zip(block_refs, keys, strict=True):
         put_block(planes[space_off], chan_off, ref[...])
-    block, size = own_ref.shape[0], own_ref.shape[0] // 2
-    pair_ref[:block, :] = own_ref[...]
-    pair_ref[block:, :] = other_ref[...]
-    first = lax.axis_index("space") == 0
+    size = own_ref.shape[0]
     half = moved.shape[0] // 2
     for source, start in ((own_ref, 0), (other_ref, half)):
         source = source[...].astype(jnp.float32)
-        source = jnp.where(first, source[:size], source[size:])
         for col_off in OFFSETS:
             cols = moved_cols(source, -col_off)
             for row_off in OFFSETS:
@@ -357,7 +374,18 @@
 
     vol_blocks = gathered(vol)
     keys = sorted(vol_blocks)
-    grad_other = from_peer(grad, 1, 0)
+    half_type = pltpu.VMEM((chan_block // 2, cells), jnp.bfloat16)
+    mine, sent, vol_blocks[0, 0] = call(
+        held_body,
+        [half_type] * 2 + [pltpu.VMEM((chan_block, cells), jnp.bfloat16)],
+        [pltpu.SemaphoreType.DMA((3,))],
+        0,
+        grad,
+        vol,
+        in_place=2,
+    )
+    other_mine = from_peer(sent, 1, 0)
+    other_rest = from_peer(mine, 1, 0)
 
     around = len(OFFSETS) ** 2
     taps = around * chan_block
@@ -379,16 +407,17 @@
         weights,
         in_place=1,
     )
-    *parts, own_plane, other_plane, pair = call(
+    *parts, own_plane, other_plane = call(
         functools.partial(kernel_grad_body, keys, rep, chunk),
-        [pltpu.VMEM((chunk, LANES), jnp.float32)] * rep
-        + [plane, plane, pltpu.VMEM((2 * chan_block, cells), jnp.bfloat16)],
+        [pltpu.VMEM((chunk, LANES), jnp.float32)] * rep + [plane, plane],
         [pltpu.VMEM((taps, cells), jnp.bfloat16), pltpu.VMEM((chunk * rep, LANES), jnp.float32)],
         flops,
         *[vol_blocks[k] for k in keys],
-        grad,
-        grad_other,
-    )
+        mine,
+        other_mine,
+    )
+    pair_type = pltpu.VMEM((2 * chan_block, cells), jnp.bfloat16)
+    pair = call(pair_body, pair_type, [], 0, mine, sent, other_mine, other_rest)
     received = [parts[0]]
     for k in range(1, rep):
         received.append(lax.ppermute(parts[k], "rep", xor_pairs(rep, k)))

time: 43.2 us -> 44.9 us (1.039)
  waiting for transfers between devices: 11.4 us -> 14.5 us
  local copies, waits for them, and re-layouts: 1.78 us -> 0 us
  Pallas kernels: 8.39 us -> 9.38 us
  starting transfers between devices: 20.7 us -> 20.1 us
    ppermute x8, waiting for transfers between devices: 0.02 us -> 1.84 us  [from_peer(): return lax.ppermute(x, 'chan', xor_pairs(peers, chan_off))]
    unnamed x4 -> x0, local copies, waits for them, and re-layouts: 1.78 us -> none
    ppermute x3, starting transfers between devices: 5.37 us -> 4.07 us  [whole_sample_layer(): spread.append(lax.ppermute(kernel_sum, 'rep', xor_pairs(rep, k)))]
    ppermute x2 -> x3, waiting for transfers between devices: 4.05 us -> 5.24 us  [from_peer(): return lax.ppermute(x, 'space', xor_pairs(2, 1))]
    pallas_call x8 -> x10, Pallas kernels: 8.39 us -> 9.38 us  [call(): pl.pallas_call(body, out_shape=out_shape, in_specs=[pl.BlockSpec(memory_s...]
    ppermute x2 -> x3, starting transfers between devices: 3.5 us -> 4.38 us  [from_peer(): return lax.ppermute(x, 'space', xor_pairs(2, 1))]
    ppermute x3, waiting for transfers between devices: 4.9 us -> 4.21 us  [whole_sample_layer(): received.append(lax.ppermute(parts[k], 'rep', xor_pairs(rep, k)))]
    ppermute x3, waiting for transfers between devices: 1.21 us -> 1.81 us  [whole_sample_layer(): spread.append(lax.ppermute(kernel_sum, 'rep', xor_pairs(rep, k)))]
  transfers between devices with their start and end apart: 19 -> 20, of which waited for: 5 -> 9; matrix products, arithmetic and copies ran while one was open for 0% -> 0% of each run, Pallas kernels for 15% -> 16%
where the time goes in v1:
time: 44.9 us; the launch traced here: 44.8 us
  starting transfers between devices  20.1 us (45%)
  waiting for transfers between devices  14.5 us (32%)
  Pallas kernels  9.38 us (21%)
  between operations  0.72 us (2%)
    pallas_call x10, Pallas kernels, call(): pl.pallas_call(body, out_shape=out_shape, in_specs=[pl.BlockSpec(memory_s...  9.38 us
    ppermute x3, waiting for transfers between devices, from_peer(): return lax.ppermute(x, 'space', xor_pairs(2, 1))  5.24 us
    ppermute x8, starting transfers between devices, from_peer(): return lax.ppermute(x, 'chan', xor_pairs(peers, chan_off))  4.96 us
    ppermute x3, starting transfers between devices, whole_sample_layer(): received.append(lax.ppermute(parts[k], 'rep', xor_pairs(rep, k)))  4.45 us
    ppermute x3, starting transfers between devices, from_peer(): return lax.ppermute(x, 'space', xor_pairs(2, 1))  4.38 us
    ppermute x3, waiting for transfers between devices, whole_sample_layer(): received.append(lax.ppermute(parts[k], 'rep', xor_pairs(rep, k)))  4.21 us
    ppermute x3, starting transfers between devices, whole_sample_layer(): spread.append(lax.ppermute(kernel_sum, 'rep', xor_pairs(rep, k)))  4.07 us
    ppermute x2, starting transfers between devices, whole_sample_layer(): across += [merged, lax.ppermute(merged, 'space', xor_pairs(2, 1))]  2.24 us
  transfers between devices with their start and end apart: 20, of which 9 were waited for; matrix products, arithmetic and copies ran while one was open for 0% of the time, Pallas kernels for 16%

profile of v1, /device:TPU:0, one launch (start us, length us, event | category | flops | bytes accessed | tf_op | source)
XLA Modules:
  0.0 44.8 jit_solution(2053913757797817478)
XLA Ops:
  0.6 3.0 %collective-permute-start.1 = (bf16[48,1024]{1,0:T(8,128)(2,1)}, bf16[48,1024]{1,0:T(8,128)(2,1)S(1)}, u32[]{:S(2)}, u32[]{:S(2)}) collective-permute-start(bf16[48,1024]{1,0:T(8,128)(2,1)} %bitcast.7), channel_id=1, source_target_pairs={{0,8},{4,12},{8,0},{12,4},{1,9},{5,13},{9,1},{13,5},{2,10},{6,14},... | collective-permute-start | bytes 294920 | tf_op jit(solution)/shard_map/ppermute | solution.py:129
  3.7 1.5 %collective-permute-start.3 = (bf16[48,1024]{1,0:T(8,128)(2,1)}, bf16[48,1024]{1,0:T(8,128)(2,1)S(1)}, u32[]{:S(2)}, u32[]{:S(2)}) collective-permute-start(bf16[48,1024]{1,0:T(8,128)(2,1)} %bitcast.8), channel_id=1, source_target_pairs={{0,16},{16,0},{1,17},{17,1},{2,18},{18,2},{3,19},{19,3},{4,20},{20... | collective-permute-start | bytes 294920 | tf_op jit(solution)/shard_map/ppermute | solution.py:131
  5.2 0.0 collective-permute-start.5
  5.2 1.8 %collective-permute-done.1.refs_2_ = bf16[48,1024]{1,0:T(8,128)(2,1)S(1)} collective-permute-done((bf16[48,1024]{1,0:T(8,128)(2,1)}, bf16[48,1024]{1,0:T(8,128)(2,1)S(1)}, u32[]{:S(2)}, u32[]{:S(2)}) %collective-permute-start.1) | collective-permute-done | bytes 98336 | tf_op jit(solution)/shard_map/ppermute | solution.py:129
  7.0 2.5 %collective-permute-done.3.refs_4_ = bf16[48,1024]{1,0:T(8,128)(2,1)S(1)} collective-permute-done((bf16[48,1024]{1,0:T(8,128)(2,1)}, bf16[48,1024]{1,0:T(8,128)(2,1)S(1)}, u32[]{:S(2)}, u32[]{:S(2)}) %collective-permute-start.3) | collective-permute-done | bytes 98336 | tf_op jit(solution)/shard_map/ppermute | solution.py:131
  9.5 1.4 %collective-permute-done.5.refs_6_ = bf16[48,1024]{1,0:T(8,128)(2,1)S(1)} collective-permute-done((bf16[48,1024]{1,0:T(8,128)(2,1)}, bf16[48,1024]{1,0:T(8,128)(2,1)S(1)}, u32[]{:S(2)}, u32[]{:S(2)}) %collective-permute-start.5) | collective-permute-done | bytes 98336 | tf_op jit(solution)/shard_map/ppermute | solution.py:133
  10.9 0.9 %shard_map.58 = (bf16[24,1024]{1,0:T(8,128)(2,1)S(1)}, bf16[24,1024]{1,0:T(8,128)(2,1)S(1)}, bf16[48,1024]{1,0:T(8,128)(2,1)S(1)}) custom-call(bf16[48,1024]{1,0:T(8,128)(2,1)} %bitcast.6, bf16[48,1024]{1,0:T(8,128)(2,1)} %bitcast.11), custom_call_target="tpu_custom_call" | custom-call | bytes 196608 | tf_op jit(solution)/shard_map/pallas_call | solution.py:353
  11.8 1.5 %collective-permute-start.7 = (bf16[24,1024]{1,0:T(8,128)(2,1)S(1)}, bf16[24,1024]{1,0:T(8,128)(2,1)S(1)}, u32[]{:S(2)}, u32[]{:S(2)}) collective-permute-start(bf16[24,1024]{1,0:T(8,128)(2,1)S(1)} %get-tuple-element.16.sent_ref), channel_id=1, source_target_pairs={{0,16},{16,0},{1,17},{17,1},{2,18},{18,2},{3,19},{19,3},{4,20},{20... | collective-permute-start | bytes 147464 | tf_op jit(solution)/shard_map/ppermute | solution.py:131
  13.3 2.7 %collective-permute-done.7.refs_9_.other_mine_ref = bf16[24,1024]{1,0:T(8,128)(2,1)S(1)} collective-permute-done((bf16[24,1024]{1,0:T(8,128)(2,1)S(1)}, bf16[24,1024]{1,0:T(8,128)(2,1)S(1)}, u32[]{:S(2)}, u32[]{:S(2)}) %collective-permute-start.7) | collective-permute-done | bytes 49184 | tf_op jit(solution)/shard_map/ppermute | solution.py:131
  16.1 1.1 %shard_map.59 = (f32[168,128]{1,0:T(8,128)S(1)}, f32[168,128]{1,0:T(8,128)S(1)}, f32[168,128]{1,0:T(8,128)S(1)}, f32[168,128]{1,0:T(8,128)S(1)}, bf16[192,1024]{...) custom-call(bf16[48,1024]{1,0:T(8,128)(2,1)S(1)} %get-tuple-element.14.refs_0_, ...), custom_call_target="tpu_custom_call" | custom-call | flops 339738624 | bytes 884736 | tf_op jit(solution)/shard_map/pallas_call | solution.py:353
  17.2 1.6 %collective-permute-start.12 = (f32[168,128]{1,0:T(8,128)S(1)}, f32[168,128]{1,0:T(8,128)S(1)}, u32[]{:S(2)}, u32[]{:S(2)}) collective-permute-start(f32[168,128]{1,0:T(8,128)S(1)} %get-tuple-element.22), channel_id=1, source_target_pairs={{0,1},{1,0},{2,3},{3,2},{4,5},{5,4},{6,7},{7,6},{8,9},{9,8},{10,11... | collective-permute-start | bytes 258056 | tf_op jit(solution)/shard_map/ppermute | solution.py:423
  18.8 1.4 %collective-permute-start.8 = (bf16[24,1024]{1,0:T(8,128)(2,1)S(1)}, bf16[24,1024]{1,0:T(8,128)(2,1)S(1)}, u32[]{:S(2)}, u32[]{:S(2)}) collective-permute-start(bf16[24,1024]{1,0:T(8,128)(2,1)S(1)} %get-tuple-element.15.refs_8_.mine_ref), channel_id=1, source_target_pairs={{0,16},{16,0},{1,17},{17,1},{2,18},{18,2},{3,19},{19,3},{4,20},{20... | collective-permute-start | bytes 147464 | tf_op jit(solution)/shard_map/ppermute | solution.py:131
  20.2 2.6 %collective-permute-start.13 = (f32[168,128]{1,0:T(8,128)S(1)}, f32[168,128]{1,0:T(8,128)S(1)}, u32[]{:S(2)}, u32[]{:S(2)}) collective-permute-start(f32[168,128]{1,0:T(8,128)S(1)} %get-tuple-element.23), channel_id=1, source_target_pairs={{0,2},{1,3},{2,0},{3,1},{4,6},{5,7},{6,4},{7,5},{8,10},{9,11},{10,... | collective-permute-start | bytes 258056 | tf_op jit(solution)/shard_map/ppermute | solution.py:423
  22.8 0.2 collective-permute-start.14
  23.0 0.1 shard_map.62.refs_0_
  23.0 0.1 collective-permute-start.9
  23.1 0.7 %collective-permute-start.10 = (bf16[96,1024]{1,0:T(8,128)(2,1)S(1)}, bf16[96,1024]{1,0:T(8,128)(2,1)S(1)}, u32[]{:S(2)}, u32[]{:S(2)}) collective-permute-start(bf16[96,1024]{1,0:T(8,128)(2,1)S(1)} %shard_map.62.refs_0_), channel_id=1, source_target_pairs={{0,8},{4,12},{8,0},{12,4},{1,9},{5,13},{9,1},{13,5},{2,10},{6,14},... | collective-permute-start | bytes 589832 | tf_op jit(solution)/shard_map/ppermute | solution.py:129
  23.8 1.2 %collective-permute-start.11 = (bf16[96,1024]{1,0:T(8,128)(2,1)S(1)}, bf16[96,1024]{1,0:T(8,128)(2,1)S(1)}, u32[]{:S(2)}, u32[]{:S(2)}) collective-permute-start(bf16[96,1024]{1,0:T(8,128)(2,1)S(1)} %shard_map.62.refs_0_), channel_id=1, source_target_pairs={{0,12},{4,8},{8,4},{12,0},{1,13},{5,9},{9,5},{13,1},{2,14},{6,10},... | collective-permute-start | bytes 589832 | tf_op jit(solution)/shard_map/ppermute | solution.py:129
  25.0 2.5 %collective-permute-done.13.refs_2_ = f32[168,128]{1,0:T(8,128)S(1)} collective-permute-done((f32[168,128]{1,0:T(8,128)S(1)}, f32[168,128]{1,0:T(8,128)S(1)}, u32[]{:S(2)}, u32[]{:S(2)}) %collective-permute-start.13) | collective-permute-done | bytes 86048 | tf_op jit(solution)/shard_map/ppermute | solution.py:423
  27.5 1.7 %collective-permute-done.14.refs_3_ = f32[168,128]{1,0:T(8,128)S(1)} collective-permute-done((f32[168,128]{1,0:T(8,128)S(1)}, f32[168,128]{1,0:T(8,128)S(1)}, u32[]{:S(2)}, u32[]{:S(2)}) %collective-permute-start.14) | collective-permute-done | bytes 86048 | tf_op jit(solution)/shard_map/ppermute | solution.py:423
  29.2 0.8 %collective-permute-start.15 = (bf16[168,128]{1,0:T(8,128)(2,1)S(1)}, bf16[168,128]{1,0:T(8,128)(2,1)S(1)}, u32[]{:S(2)}, u32[]{:S(2)}) collective-permute-start(bf16[168,128]{1,0:T(8,128)(2,1)S(1)} %shard_map.64.refs_0_), channel_id=1, source_target_pairs={{0,1},{1,0},{2,3},{3,2},{4,5},{5,4},{6,7},{7,6},{8,9},{9,8},{10,11... | collective-permute-start | bytes 129032 | tf_op jit(solution)/shard_map/ppermute | solution.py:450
  30.0 1.6 %collective-permute-start.17 = (bf16[168,128]{1,0:T(8,128)(2,1)S(1)}, bf16[168,128]{1,0:T(8,128)(2,1)S(1)}, u32[]{:S(2)}, u32[]{:S(2)}) collective-permute-start(bf16[168,128]{1,0:T(8,128)(2,1)S(1)} %shard_map.64.refs_0_), channel_id=1, source_target_pairs={{0,2},{1,3},{2,0},{3,1},{4,6},{5,7},{6,4},{7,5},{8,10},{9,11},{10,... | collective-permute-start | bytes 129032 | tf_op jit(solution)/shard_map/ppermute | solution.py:450
  31.6 1.8 %collective-permute-done.15.refs_1_ = bf16[168,128]{1,0:T(8,128)(2,1)S(1)} collective-permute-done((bf16[168,128]{1,0:T(8,128)(2,1)S(1)}, bf16[168,128]{1,0:T(8,128)(2,1)S(1)}, u32[]{:S(2)}, u32[]{:S(2)}) %collective-permute-start.15) | collective-permute-done | bytes 43040 | tf_op jit(solution)/shard_map/ppermute | solution.py:450
  33.3 1.7 %collective-permute-start.18 = (bf16[168,128]{1,0:T(8,128)(2,1)S(1)}, bf16[168,128]{1,0:T(8,128)(2,1)S(1)}, u32[]{:S(2)}, u32[]{:S(2)}) collective-permute-start(bf16[168,128]{1,0:T(8,128)(2,1)S(1)} %shard_map.64.refs_0_), channel_id=1, source_target_pairs={{0,3},{1,2},{2,1},{3,0},{4,7},{5,6},{6,5},{7,4},{8,11},{9,10},{10,... | collective-permute-start | bytes 129032 | tf_op jit(solution)/shard_map/ppermute | solution.py:450
  35.0 2.5 %shard_map.60 = (bf16[3,432,192]{2,1,0:T(8,128)(2,1)S(1)}, bf16[27,48,192]{2,1,0:T(8,128)(2,1)S(1)}) custom-call(bf16[27,192,192]{2,1,0:T(8,128)(2,1)} %weight_ref.1), custom_call_target="tpu_custom_call" | custom-call | flops 95551488 | bytes 1990656 | tf_op jit(solution)/shard_map/pallas_call | solution.py:353
  37.5 1.5 %collective-permute-start.16 = (bf16[336,128]{1,0:T(8,128)(2,1)S(1)}, bf16[336,128]{1,0:T(8,128)(2,1)S(1)}, u32[]{:S(2)}, u32[]{:S(2)}) collective-permute-start(bf16[336,128]{1,0:T(8,128)(2,1)S(1)} %shard_map.65.near_ref), channel_id=1, source_target_pairs={{0,16},{16,0},{1,17},{17,1},{2,18},{18,2},{3,19},{19,3},{4,20},{20... | collective-permute-start | bytes 258056 | tf_op jit(solution)/shard_map/ppermute | solution.py:455
  39.1 0.1 collective-permute-done.18.refs_1_
  39.1 0.7 %collective-permute-start.19 = (bf16[336,128]{1,0:T(8,128)(2,1)S(1)}, bf16[336,128]{1,0:T(8,128)(2,1)S(1)}, u32[]{:S(2)}, u32[]{:S(2)}) collective-permute-start(bf16[336,128]{1,0:T(8,128)(2,1)S(1)} %shard_map.66.far_ref), channel_id=1, source_target_pairs={{0,16},{16,0},{1,17},{17,1},{2,18},{18,2},{3,19},{19,3},{4,20},{20... | collective-permute-start | bytes 258056 | tf_op jit(solution)/shard_map/ppermute | solution.py:455
  39.8 1.8 %shard_map.61 = bf16[48,1024]{1,0:T(8,128)(2,1)} custom-call(bf16[192,1024]{1,0:T(8,128)(2,1)S(1)} %get-tuple-element.17.own_plane, bf16[192,1024]{1,0:T(8,128)(2,1)S(1)} %get-tuple-element.18.other_plane, bf16[3,432,192]{2,1,0:T(8,128)(2,1)S(1)} %get-tuple-element.19.weight_ref), custom_call_target="tpu_custom_call" | custom-call | flops 509607936 | bytes 1284096 | tf_op jit(solution)/shard_map/pallas_call | solution.py:353
  41.7 1.9 %shard_map.63 = bf16[48,1024]{1,0:T(8,128)(2,1)} custom-call(bf16[96,1024]{1,0:T(8,128)(2,1)S(1)} %shard_map.62.refs_0_, bf16[96,1024]{1,0:T(8,128)(2,1)S(1)} %collective-permute-done.9.refs_1_, bf16[96,1024]{1,0:T(8,128)(2,1)S(1)} %collective-permute-done.10.refs_2_, bf16[96,1024]{1,0:T(8,128)(2,1)S(1)} %collective-permute-done.11.refs_3_, ...), custom_call_target="tpu_custom_call" | custom-call | flops 509607936 | bytes 1284096 | tf_op jit(solution)/shard_map/pallas_call | solution.py:353
  43.6 0.1 collective-permute-done.19.far_other_ref
  43.7 1.1 %shard_map.67 = bf16[27,48,192]{2,1,0:T(8,128)(2,1)} custom-call(bf16[336,128]{1,0:T(8,128)(2,1)S(1)} %shard_map.65.near_ref, bf16[336,128]{1,0:T(8,128)(2,1)S(1)} %collective-permute-done.16.near_other_ref, bf16[336,128]{1,0:T(8,128)(2,1)S(1)} %shard_map.66.far_ref, bf16[336,128]{1,0:T(8,128)(2,1)S(1)} %collective-permute-done.19.far_other_ref), custom_call_target="tpu_custom_call" | custom-call | bytes 344064 | tf_op jit(solution)/shard_map/pallas_call | solution.py:353
  (18 shorter events, 0.1 us)
Async XLA Ops:
  0.6 6.4 %collective-permute-start.1 = (bf16[48,1024]{1,0:T(8,128)(2,1)}, bf16[48,1024]{1,0:T(8,128)(2,1)S(1)}, u32[]{:S(2)}, u32[]{:S(2)}) collective-permute-start(bf16[48,1024]{1,0:T(8,128)(2,1)} %bitcast.7), channel_id=1, source_target_pairs={{0,8},{4,12},{8,0},{12,4},{1,9},{5,13},{9,1},{13,5},{2,10},{6,14},... | collective-permute-start | bytes 294920 | tf_op jit(solution)/shard_map/ppermute | solution.py:129
  3.7 5.9 %collective-permute-start.3 = (bf16[48,1024]{1,0:T(8,128)(2,1)}, bf16[48,1024]{1,0:T(8,128)(2,1)S(1)}, u32[]{:S(2)}, u32[]{:S(2)}) collective-permute-start(bf16[48,1024]{1,0:T(8,128)(2,1)} %bitcast.8), channel_id=1, source_target_pairs={{0,16},{16,0},{1,17},{17,1},{2,18},{18,2},{3,19},{19,3},{4,20},{20... | collective-permute-start | bytes 294920 | tf_op jit(solution)/shard_map/ppermute | solution.py:131
  5.2 5.7 %collective-permute-start.5 = (bf16[48,1024]{1,0:T(8,128)(2,1)}, bf16[48,1024]{1,0:T(8,128)(2,1)S(1)}, u32[]{:S(2)}, u32[]{:S(2)}) collective-permute-start(bf16[48,1024]{1,0:T(8,128)(2,1)} %bitcast.9), channel_id=1, source_target_pairs={{0,24},{4,28},{8,16},{12,20},{16,8},{20,12},{24,0},{28,4},{1,25},{... | collective-permute-start | bytes 294920 | tf_op jit(solution)/shard_map/ppermute | solution.py:133
  5.2 10.9 %collective-permute-start = (bf16[48,1024]{1,0:T(8,128)(2,1)}, bf16[48,1024]{1,0:T(8,128)(2,1)S(1)}, u32[]{:S(2)}, u32[]{:S(2)}) collective-permute-start(bf16[48,1024]{1,0:T(8,128)(2,1)} %bitcast.10), channel_id=1, source_target_pairs={{0,4},{4,0},{8,12},{12,8},{1,5},{5,1},{9,13},{13,9},{2,6},{6,2},{1... | collective-permute-start | bytes 294920 | tf_op jit(solution)/shard_map/ppermute | solution.py:129
  7.0 9.0 %collective-permute-start.2 = (bf16[48,1024]{1,0:T(8,128)(2,1)S(1)}, bf16[48,1024]{1,0:T(8,128)(2,1)S(1)}, u32[]{:S(2)}, u32[]{:S(2)}) collective-permute-start(bf16[48,1024]{1,0:T(8,128)(2,1)S(1)} %collective-permute-done.1.refs_2_), channel_id=1, source_target_pairs={{0,4},{4,0},{8,12},{12,8},{1,5},{5,1},{9,13},{13,9},{2,6},{6,2},{1... | collective-permute-start | bytes 294920 | tf_op jit(solution)/shard_map/ppermute | solution.py:129
  9.5 6.5 %collective-permute-start.4 = (bf16[48,1024]{1,0:T(8,128)(2,1)S(1)}, bf16[48,1024]{1,0:T(8,128)(2,1)S(1)}, u32[]{:S(2)}, u32[]{:S(2)}) collective-permute-start(bf16[48,1024]{1,0:T(8,128)(2,1)S(1)} %collective-permute-done.3.refs_4_), channel_id=1, source_target_pairs={{0,4},{4,0},{8,12},{12,8},{1,5},{5,1},{9,13},{13,9},{2,6},{6,2},{1... | collective-permute-start | bytes 294920 | tf_op jit(solution)/shard_map/ppermute | solution.py:129
  10.9 5.2 %collective-permute-start.6 = (bf16[48,1024]{1,0:T(8,128)(2,1)S(1)}, bf16[48,1024]{1,0:T(8,128)(2,1)S(1)}, u32[]{:S(2)}, u32[]{:S(2)}) collective-permute-start(bf16[48,1024]{1,0:T(8,128)(2,1)S(1)} %collective-permute-done.5.refs_6_), channel_id=1, source_target_pairs={{0,4},{4,0},{8,12},{12,8},{1,5},{5,1},{9,13},{13,9},{2,6},{6,2},{1... | collective-permute-start | bytes 294920 | tf_op jit(solution)/shard_map/ppermute | solution.py:129
  11.8 4.2 %collective-permute-start.7 = (bf16[24,1024]{1,0:T(8,128)(2,1)S(1)}, bf16[24,1024]{1,0:T(8,128)(2,1)S(1)}, u32[]{:S(2)}, u32[]{:S(2)}) collective-permute-start(bf16[24,1024]{1,0:T(8,128)(2,1)S(1)} %get-tuple-element.16.sent_ref), channel_id=1, source_target_pairs={{0,16},{16,0},{1,17},{17,1},{2,18},{18,2},{3,19},{19,3},{4,20},{20... | collective-permute-start | bytes 147464 | tf_op jit(solution)/shard_map/ppermute | solution.py:131
  17.2 6.6 %collective-permute-start.12 = (f32[168,128]{1,0:T(8,128)S(1)}, f32[168,128]{1,0:T(8,128)S(1)}, u32[]{:S(2)}, u32[]{:S(2)}) collective-permute-start(f32[168,128]{1,0:T(8,128)S(1)} %get-tuple-element.22), channel_id=1, source_target_pairs={{0,1},{1,0},{2,3},{3,2},{4,5},{5,4},{6,7},{7,6},{8,9},{9,8},{10,11... | collective-permute-start | bytes 258056 | tf_op jit(solution)/shard_map/ppermute | solution.py:423
  18.8 4.2 %collective-permute-start.8 = (bf16[24,1024]{1,0:T(8,128)(2,1)S(1)}, bf16[24,1024]{1,0:T(8,128)(2,1)S(1)}, u32[]{:S(2)}, u32[]{:S(2)}) collective-permute-start(bf16[24,1024]{1,0:T(8,128)(2,1)S(1)} %get-tuple-element.15.refs_8_.mine_ref), channel_id=1, source_target_pairs={{0,16},{16,0},{1,17},{17,1},{2,18},{18,2},{3,19},{19,3},{4,20},{20... | collective-permute-start | bytes 147464 | tf_op jit(solution)/shard_map/ppermute | solution.py:131
  20.2 7.3 %collective-permute-start.13 = (f32[168,128]{1,0:T(8,128)S(1)}, f32[168,128]{1,0:T(8,128)S(1)}, u32[]{:S(2)}, u32[]{:S(2)}) collective-permute-start(f32[168,128]{1,0:T(8,128)S(1)} %get-tuple-element.23), channel_id=1, source_target_pairs={{0,2},{1,3},{2,0},{3,1},{4,6},{5,7},{6,4},{7,5},{8,10},{9,11},{10,... | collective-permute-start | bytes 258056 | tf_op jit(solution)/shard_map/ppermute | solution.py:423
  22.8 6.4 %collective-permute-start.14 = (f32[168,128]{1,0:T(8,128)S(1)}, f32[168,128]{1,0:T(8,128)S(1)}, u32[]{:S(2)}, u32[]{:S(2)}) collective-permute-start(f32[168,128]{1,0:T(8,128)S(1)} %get-tuple-element.24), channel_id=1, source_target_pairs={{0,3},{1,2},{2,1},{3,0},{4,7},{5,6},{6,5},{7,4},{8,11},{9,10},{10,... | collective-permute-start | bytes 258056 | tf_op jit(solution)/shard_map/ppermute | solution.py:423
  23.0 18.6 %collective-permute-start.9 = (bf16[96,1024]{1,0:T(8,128)(2,1)S(1)}, bf16[96,1024]{1,0:T(8,128)(2,1)S(1)}, u32[]{:S(2)}, u32[]{:S(2)}) collective-permute-start(bf16[96,1024]{1,0:T(8,128)(2,1)S(1)} %shard_map.62.refs_0_), channel_id=1, source_target_pairs={{0,4},{4,0},{8,12},{12,8},{1,5},{5,1},{9,13},{13,9},{2,6},{6,2},{1... | collective-permute-start | bytes 589832 | tf_op jit(solution)/shard_map/ppermute | solution.py:129
  23.1 18.6 %collective-permute-start.10 = (bf16[96,1024]{1,0:T(8,128)(2,1)S(1)}, bf16[96,1024]{1,0:T(8,128)(2,1)S(1)}, u32[]{:S(2)}, u32[]{:S(2)}) collective-permute-start(bf16[96,1024]{1,0:T(8,128)(2,1)S(1)} %shard_map.62.refs_0_), channel_id=1, source_target_pairs={{0,8},{4,12},{8,0},{12,4},{1,9},{5,13},{9,1},{13,5},{2,10},{6,14},... | collective-permute-start | bytes 589832 | tf_op jit(solution)/shard_map/ppermute | solution.py:129
  23.8 17.9 %collective-permute-start.11 = (bf16[96,1024]{1,0:T(8,128)(2,1)S(1)}, bf16[96,1024]{1,0:T(8,128)(2,1)S(1)}, u32[]{:S(2)}, u32[]{:S(2)}) collective-permute-start(bf16[96,1024]{1,0:T(8,128)(2,1)S(1)} %shard_map.62.refs_0_), channel_id=1, source_target_pairs={{0,12},{4,8},{8,4},{12,0},{1,13},{5,9},{9,5},{13,1},{2,14},{6,10},... | collective-permute-start | bytes 589832 | tf_op jit(solution)/shard_map/ppermute | solution.py:129
  29.2 4.1 %collective-permute-start.15 = (bf16[168,128]{1,0:T(8,128)(2,1)S(1)}, bf16[168,128]{1,0:T(8,128)(2,1)S(1)}, u32[]{:S(2)}, u32[]{:S(2)}) collective-permute-start(bf16[168,128]{1,0:T(8,128)(2,1)S(1)} %shard_map.64.refs_0_), channel_id=1, source_target_pairs={{0,1},{1,0},{2,3},{3,2},{4,5},{5,4},{6,7},{7,6},{8,9},{9,8},{10,11... | collective-permute-start | bytes 129032 | tf_op jit(solution)/shard_map/ppermute | solution.py:450
  30.0 7.5 %collective-permute-start.17 = (bf16[168,128]{1,0:T(8,128)(2,1)S(1)}, bf16[168,128]{1,0:T(8,128)(2,1)S(1)}, u32[]{:S(2)}, u32[]{:S(2)}) collective-permute-start(bf16[168,128]{1,0:T(8,128)(2,1)S(1)} %shard_map.64.refs_0_), channel_id=1, source_target_pairs={{0,2},{1,3},{2,0},{3,1},{4,6},{5,7},{6,4},{7,5},{8,10},{9,11},{10,... | collective-permute-start | bytes 129032 | tf_op jit(solution)/shard_map/ppermute | solution.py:450
  33.3 5.8 %collective-permute-start.18 = (bf16[168,128]{1,0:T(8,128)(2,1)S(1)}, bf16[168,128]{1,0:T(8,128)(2,1)S(1)}, u32[]{:S(2)}, u32[]{:S(2)}) collective-permute-start(bf16[168,128]{1,0:T(8,128)(2,1)S(1)} %shard_map.64.refs_0_), channel_id=1, source_target_pairs={{0,3},{1,2},{2,1},{3,0},{4,7},{5,6},{6,5},{7,4},{8,11},{9,10},{10,... | collective-permute-start | bytes 129032 | tf_op jit(solution)/shard_map/ppermute | solution.py:450
  37.5 6.0 %collective-permute-start.16 = (bf16[336,128]{1,0:T(8,128)(2,1)S(1)}, bf16[336,128]{1,0:T(8,128)(2,1)S(1)}, u32[]{:S(2)}, u32[]{:S(2)}) collective-permute-start(bf16[336,128]{1,0:T(8,128)(2,1)S(1)} %shard_map.65.near_ref), channel_id=1, source_target_pairs={{0,16},{16,0},{1,17},{17,1},{2,18},{18,2},{3,19},{19,3},{4,20},{20... | collective-permute-start | bytes 258056 | tf_op jit(solution)/shard_map/ppermute | solution.py:455
  39.1 4.5 %collective-permute-start.19 = (bf16[336,128]{1,0:T(8,128)(2,1)S(1)}, bf16[336,128]{1,0:T(8,128)(2,1)S(1)}, u32[]{:S(2)}, u32[]{:S(2)}) collective-permute-start(bf16[336,128]{1,0:T(8,128)(2,1)S(1)} %shard_map.66.far_ref), channel_id=1, source_target_pairs={{0,16},{16,0},{1,17},{17,1},{2,18},{18,2},{3,19},{19,3},{4,20},{20... | collective-permute-start | bytes 258056 | tf_op jit(solution)/shard_map/ppermute | solution.py:455

commit v2 on v1

--- a/solution.py
+++ b/solution.py
@@ -291,24 +291,34 @@
     out_ref[...] = out.astype(out_ref.dtype)
 
 
-def forward_body(own_plane, other_plane, weight_ref, out_ref):
-    convolve(1, lambda depth_off: weight_ref[depth_off + 1], own_plane, other_plane, out_ref)
-
-
-def backward_body(keys, *refs):
-    pair_refs = refs[: len(keys)]
-    weight_ref, out_ref, own_plane, other_plane = refs[len(keys) :]
-    size, channels = out_ref.shape[0], weight_ref.shape[2]
+def convolutions_body(keys, chunk, *refs):
+    pair_refs, refs = refs[: len(keys)], refs[len(keys) :]
+    backward_ref, own_vol, other_vol, forward_ref, near_ref, far_ref = refs[:6]
+    grad_in_ref, conv_ref, kernel_ref = refs[6:9]
+    own_plane, other_plane, held, sems, packed, taps_held, taps_sems = refs[9:]
+    y = lax.axis_index("space")
+    copies = start_half(chunk, y, (near_ref, far_ref), kernel_ref, packed, taps_held, taps_sems)
+    size, channels = conv_ref.shape[0], backward_ref.shape[2]
     taps = len(OFFSETS) ** 2
     for ref, chan_off in zip(pair_refs, keys, strict=True):
         put_block(own_plane, chan_off, ref[:size, :])
         put_block(other_plane, chan_off, ref[size:, :])
 
-    def weights_of(depth_off):
-        rows = weight_ref[(depth_off + 1) * taps : (depth_off + 2) * taps]
+    def backward_of(depth_off):
+        rows = backward_ref[(depth_off + 1) * taps : (depth_off + 2) * taps]
         return rows.reshape(taps * size, channels)
 
-    convolve(-1, weights_of, own_plane, other_plane, out_ref)
+    def forward_of(depth_off):
+        return forward_ref[depth_off + 1]
+
+    for i, (sign, weights_of, planes, out_ref) in enumerate(
+        ((1, forward_of, (own_vol, other_vol), conv_ref), (-1, backward_of, (own_plane, other_plane), grad_in_ref))
+    ):
+        convolve(sign, weights_of, *planes, held.at[i])
+        copies.append(pltpu.make_async_copy(held.at[i], out_ref, sems.at[i]))
+        copies[-1].start()
+    for copy in copies:
+        copy.wait()
 
 
 def merge_body(*refs):
@@ -318,33 +328,42 @@
         out_ref[i * size : (i + 1) * size, :] = ref[...]
 
 
-def assemble_body(chunk, near_ref, near_other_ref, far_ref, far_other_ref, out_ref, packed):
-    space, mine = lax.axis_index("space"), lax.axis_index("rep")
-    for y, refs in ((space, (near_ref, far_ref)), (space ^ 1, (near_other_ref, far_other_ref))):
-        k = 0
-        for ref in refs:
-            for start in range(0, ref.shape[0], chunk):
-                at = pl.multiple_of((mine ^ k) * chunk, SUBLANES)
-                packed[y, pl.ds(at, chunk), :] = ref[start : start + chunk, :].astype(jnp.float32)
-                k += 1
-    size = out_ref.shape[1] // 2
-    around = len(OFFSETS) ** 2
+def start_half(chunk, y, refs, out_ref, packed, held, sems):
+    mine = lax.axis_index("rep")
+    k = 0
+    for ref in refs:
+        for start in range(0, ref.shape[0], chunk):
+            at = pl.multiple_of((mine ^ k) * chunk, SUBLANES)
+            packed[pl.ds(at, chunk), :] = ref[start : start + chunk, :].astype(jnp.float32)
+            k += 1
+    _, around, size, _ = held.shape
     half = size * around
-    for depth_off in OFFSETS:
-        held = abs(depth_off)
+    rows = pl.ds(pl.multiple_of(y * size, SUBLANES), size)
+    copies = []
+    for plane in (1, 0):
         for i in range(around):
-            tap = (depth_off + 1) * around + i
-            for y in (0, 1):
-                rows = slice(y * size, (y + 1) * size)
-                at = held * half + i * size
-                out_ref[tap, rows, :LANES] = packed[y, at : at + size, :].astype(out_ref.dtype)
-                at = 2 * half + i * size
-                lanes = slice(held * LANES // 2, (held + 1) * LANES // 2)
-                out_ref[tap, rows, LANES:] = packed[y, at : at + size, lanes].astype(out_ref.dtype)
-
-
-def call(body, out_shape, scratch, flops, *operands, in_place=0):
-    in_vmem = pl.BlockSpec(memory_space=pltpu.VMEM)
+            at = plane * half + i * size
+            held[plane, i, :, :LANES] = packed[at : at + size, :].astype(held.dtype)
+            at = 2 * half + i * size
+            lanes = slice(plane * LANES // 2, (plane + 1) * LANES // 2)
+            held[plane, i, :, LANES:] = packed[at : at + size, lanes].astype(held.dtype)
+        for depth_off in OFFSETS:
+            if abs(depth_off) == plane:
+                depth = depth_off + 1
+                part = out_ref.at[pl.ds(depth * around, around), rows]
+                copies.append(pltpu.make_async_copy(held.at[plane], part, sems.at[depth]))
+                copies[-1].start()
+    return copies
+
+
+def assemble_body(chunk, half_out_ref, near_ref, far_ref, out_ref, packed, held, sems):
+    del half_out_ref
+    y = lax.axis_index("space") ^ 1
+    for copy in start_half(chunk, y, (near_ref, far_ref), out_ref, packed, held, sems):
+        copy.wait()
+
+
+def call(body, out_shape, scratch, flops, *operands, in_place=0, out_space=pltpu.VMEM, aliases=()):
     spaces = [pltpu.HBM] * in_place + [pltpu.VMEM] * (len(operands) - in_place)
     operands = [
         pltpu.with_memory_space_constraint(x, space)
@@ -354,8 +373,9 @@
         body,
         out_shape=out_shape,
         in_specs=[pl.BlockSpec(memory_space=space) for space in spaces],
-        out_specs=jax.tree.map(lambda _: in_vmem, out_shape),
+        out_specs=jax.tree.map(lambda _: pl.BlockSpec(memory_space=out_space), out_shape),
         scratch_shapes=scratch,
+        input_output_aliases=dict(aliases),
         compiler_params=pltpu.CompilerParams(vmem_limit_bytes=KERNEL_VMEM),
         cost_estimate=pl.CostEstimate(
             flops=flops,
@@ -433,18 +453,6 @@
     grad_pairs = gathered_pairs(pair)
     pair_keys = sorted(grad_pairs)
     out_type = jax.ShapeDtypeStruct((chan_block, cells), jnp.bfloat16)
-    conv_out = call(
-        forward_body, out_type, [], 3 * flops // 2, own_plane, other_plane, forward_weights
-    )
-    grad_in = call(
-        functools.partial(backward_body, pair_keys),
-        out_type,
-        [plane, plane],
-        3 * flops // 2,
-        *[grad_pairs[k] for k in pair_keys],
-        backward_weights,
-    )
-
     spread = [kernel_sum]
     for k in range(1, rep):
         spread.append(lax.ppermute(kernel_sum, "rep", xor_pairs(rep, k)))
@@ -452,13 +460,45 @@
     for held in (spread[:2], spread[2:]):
         merged_type = pltpu.VMEM((len(held) * chunk, LANES), jnp.bfloat16)
         merged = call(merge_body, merged_type, [], 0, *held)
-        across += [merged, lax.ppermute(merged, "space", xor_pairs(2, 1))]
+        across.append((merged, lax.ppermute(merged, "space", xor_pairs(2, 1))))
+    (near, near_other), (far, far_other) = across
+    kernel_type = jax.ShapeDtypeStruct((weights.shape[0], chan_block, channels), jnp.bfloat16)
+    half_scratch = [
+        pltpu.VMEM((chunk * rep, LANES), jnp.float32),
+        pltpu.VMEM((space, around, chan_block // 2, channels), jnp.bfloat16),
+        pltpu.SemaphoreType.DMA((len(OFFSETS),)),
+    ]
+    grad_in, conv_out, kernel_half = call(
+        functools.partial(convolutions_body, pair_keys, chunk),
+        [out_type, out_type, kernel_type],
+        [
+            plane,
+            plane,
+            pltpu.VMEM((2, chan_block, cells), jnp.bfloat16),
+            pltpu.SemaphoreType.DMA((2,)),
+            *half_scratch,
+        ],
+        3 * flops,
+        *[grad_pairs[k] for k in pair_keys],
+        backward_weights,
+        own_plane,
+        other_plane,
+        forward_weights,
+        near,
+        far,
+        out_space=pltpu.HBM,
+    )
     grad_weights = call(
         functools.partial(assemble_body, chunk),
-        jax.ShapeDtypeStruct((weights.shape[0], chan_block, channels), jnp.bfloat16),
-        [pltpu.VMEM((space, chunk * rep, LANES), jnp.float32)],
+        kernel_type,
+        half_scratch,
         0,
-        *across,
+        kernel_half,
+        near_other,
+        far_other,
+        in_place=1,
+        out_space=pltpu.HBM,
+        aliases={0: 0},
     )
     return (
         conv_out.reshape(volume.shape),

time: 44.9 us -> 50.3 us (1.12)
  waiting for transfers between devices: 14.5 us -> 19.7 us
  starting transfers between devices: 20.1 us -> 21.6 us
  Pallas kernels: 9.38 us -> 8.13 us
    ppermute x1, starting transfers between devices: 0.02 us -> 3.99 us  [from_peer(): return lax.ppermute(x, ('space', 'chan'), pairs)]
    ppermute x3, starting transfers between devices: 4.38 us -> 1.98 us  [from_peer(): return lax.ppermute(x, 'space', xor_pairs(2, 1))]
    ppermute x3, waiting for transfers between devices: 4.21 us -> 6.51 us  [whole_sample_layer(): received.append(lax.ppermute(parts[k], 'rep', xor_pairs(rep, k)))]
    ppermute x3, starting transfers between devices: 4.07 us -> 6.1 us  [whole_sample_layer(): spread.append(lax.ppermute(kernel_sum, 'rep', xor_pairs(rep, k)))]
    ppermute x8, starting transfers between devices: 4.96 us -> 2.97 us  [from_peer(): return lax.ppermute(x, 'chan', xor_pairs(peers, chan_off))]
    ppermute x1, waiting for transfers between devices: 1.36 us -> 3.07 us  [from_peer(): return lax.ppermute(x, ('space', 'chan'), pairs)]
    pallas_call x10 -> x9, Pallas kernels: 9.38 us -> 8.13 us  [call(): pl.pallas_call(body, out_shape=out_shape, in_specs=[pl.BlockSpec(memory_s...]
    ppermute x3, waiting for transfers between devices: 5.24 us -> 6.37 us  [from_peer(): return lax.ppermute(x, 'space', xor_pairs(2, 1))]
  transfers between devices with their start and end apart: 20 -> 20, of which waited for: 9 -> 8; matrix products, arithmetic and copies ran while one was open for 0% -> 0% of each run, Pallas kernels for 16% -> 12%
where the time goes in v2:
time: 50.3 us; the launch traced here: 50.2 us
  starting transfers between devices  21.6 us (43%)
  waiting for transfers between devices  19.7 us (39%)
  Pallas kernels  8.13 us (16%)
  between operations  0.72 us (1%)
    pallas_call x9, Pallas kernels, call(): pl.pallas_call(body, out_shape=out_shape, in_specs=[pl.BlockSpec(memory_s...  8.13 us
    ppermute x3, waiting for transfers between devices, whole_sample_layer(): received.append(lax.ppermute(parts[k], 'rep', xor_pairs(rep, k)))  6.51 us
    ppermute x3, waiting for transfers between devices, from_peer(): return lax.ppermute(x, 'space', xor_pairs(2, 1))  6.37 us
    ppermute x3, starting transfers between devices, whole_sample_layer(): spread.append(lax.ppermute(kernel_sum, 'rep', xor_pairs(rep, k)))  6.1 us
    ppermute x3, starting transfers between devices, whole_sample_layer(): received.append(lax.ppermute(parts[k], 'rep', xor_pairs(rep, k)))  4.45 us
    ppermute x1, starting transfers between devices, from_peer(): return lax.ppermute(x, ('space', 'chan'), pairs)  3.99 us
    ppermute x1, waiting for transfers between devices, from_peer(): return lax.ppermute(x, ('space', 'chan'), pairs)  3.07 us
    ppermute x8, starting transfers between devices, from_peer(): return lax.ppermute(x, 'chan', xor_pairs(peers, chan_off))  2.97 us
  transfers between devices with their start and end apart: 20, of which 8 were waited for; matrix products, arithmetic and copies ran while one was open for 0% of the time, Pallas kernels for 12%

profile of v2, /device:TPU:0, one launch (start us, length us, event | category | flops | bytes accessed | tf_op | source)
XLA Modules:
  0.0 50.2 jit_solution(2070890758334023592)
XLA Ops:
  0.6 4.0 %collective-permute-start.10 = (bf16[48,1024]{1,0:T(8,128)(2,1)}, bf16[48,1024]{1,0:T(8,128)(2,1)S(1)}, u32[]{:S(2)}, u32[]{:S(2)}) collective-permute-start(bf16[48,1024]{1,0:T(8,128)(2,1)} %bitcast.7), channel_id=1, source_target_pairs={{0,24},{4,28},{8,16},{12,20},{16,8},{20,12},{24,0},{28,4},{1,25},{... | collective-permute-start | bytes 294920 | tf_op jit(solution)/shard_map/ppermute | solution.py:133
  4.6 0.5 %collective-permute-start.6 = (bf16[48,1024]{1,0:T(8,128)(2,1)}, bf16[48,1024]{1,0:T(8,128)(2,1)S(1)}, u32[]{:S(2)}, u32[]{:S(2)}) collective-permute-start(bf16[48,1024]{1,0:T(8,128)(2,1)} %bitcast.8), channel_id=1, source_target_pairs={{0,8},{4,12},{8,0},{12,4},{1,9},{5,13},{9,1},{13,5},{2,10},{6,14},... | collective-permute-start | bytes 294920 | tf_op jit(solution)/shard_map/ppermute | solution.py:129
  5.2 0.1 collective-permute-start.8
  5.3 0.0 collective-permute-start.5
  5.3 3.1 %collective-permute-done.10.refs_6_ = bf16[48,1024]{1,0:T(8,128)(2,1)S(1)} collective-permute-done((bf16[48,1024]{1,0:T(8,128)(2,1)}, bf16[48,1024]{1,0:T(8,128)(2,1)S(1)}, u32[]{:S(2)}, u32[]{:S(2)}) %collective-permute-start.10) | collective-permute-done | bytes 98336 | tf_op jit(solution)/shard_map/ppermute | solution.py:133
  8.3 1.7 %collective-permute-done.6.refs_2_ = bf16[48,1024]{1,0:T(8,128)(2,1)S(1)} collective-permute-done((bf16[48,1024]{1,0:T(8,128)(2,1)}, bf16[48,1024]{1,0:T(8,128)(2,1)S(1)}, u32[]{:S(2)}, u32[]{:S(2)}) %collective-permute-start.6) | collective-permute-done | bytes 98336 | tf_op jit(solution)/shard_map/ppermute | solution.py:129
  10.1 0.5 %collective-permute-start.9 = (bf16[48,1024]{1,0:T(8,128)(2,1)S(1)}, bf16[48,1024]{1,0:T(8,128)(2,1)S(1)}, u32[]{:S(2)}, u32[]{:S(2)}) collective-permute-start(bf16[48,1024]{1,0:T(8,128)(2,1)S(1)} %collective-permute-done.8.refs_4_), channel_id=1, source_target_pairs={{0,4},{4,0},{8,12},{12,8},{1,5},{5,1},{9,13},{13,9},{2,6},{6,2},{1... | collective-permute-start | bytes 294920 | tf_op jit(solution)/shard_map/ppermute | solution.py:129
  10.6 0.9 %shard_map.58 = (bf16[24,1024]{1,0:T(8,128)(2,1)S(1)}, bf16[24,1024]{1,0:T(8,128)(2,1)S(1)}, bf16[48,1024]{1,0:T(8,128)(2,1)S(1)}) custom-call(bf16[48,1024]{1,0:T(8,128)(2,1)} %bitcast.6, bf16[48,1024]{1,0:T(8,128)(2,1)} %bitcast.11), custom_call_target="tpu_custom_call" | custom-call | bytes 196608 | tf_op jit(solution)/shard_map/pallas_call | solution.py:372
  11.5 0.9 %collective-permute-start = (bf16[24,1024]{1,0:T(8,128)(2,1)S(1)}, bf16[24,1024]{1,0:T(8,128)(2,1)S(1)}, u32[]{:S(2)}, u32[]{:S(2)}) collective-permute-start(bf16[24,1024]{1,0:T(8,128)(2,1)S(1)} %get-tuple-element.18.sent_ref), channel_id=1, source_target_pairs={{0,16},{16,0},{1,17},{17,1},{2,18},{18,2},{3,19},{19,3},{4,20},{20... | collective-permute-start | bytes 147464 | tf_op jit(solution)/shard_map/ppermute | solution.py:131
  12.4 3.2 %collective-permute-done.other_mine_ref.refs_9_ = bf16[24,1024]{1,0:T(8,128)(2,1)S(1)} collective-permute-done((bf16[24,1024]{1,0:T(8,128)(2,1)S(1)}, bf16[24,1024]{1,0:T(8,128)(2,1)S(1)}, u32[]{:S(2)}, u32[]{:S(2)}) %collective-permute-start) | collective-permute-done | bytes 49184 | tf_op jit(solution)/shard_map/ppermute | solution.py:131
  15.7 1.1 %shard_map.61 = (f32[168,128]{1,0:T(8,128)S(1)}, f32[168,128]{1,0:T(8,128)S(1)}, f32[168,128]{1,0:T(8,128)S(1)}, f32[168,128]{1,0:T(8,128)S(1)}, bf16[192,1024]{...) custom-call(bf16[48,1024]{1,0:T(8,128)(2,1)S(1)} %get-tuple-element.20.refs_0_, ...), custom_call_target="tpu_custom_call" | custom-call | flops 339738624 | bytes 884736 | tf_op jit(solution)/shard_map/pallas_call | solution.py:372
  16.8 1.6 %collective-permute-start.12 = (f32[168,128]{1,0:T(8,128)S(1)}, f32[168,128]{1,0:T(8,128)S(1)}, u32[]{:S(2)}, u32[]{:S(2)}) collective-permute-start(f32[168,128]{1,0:T(8,128)S(1)} %get-tuple-element.25), channel_id=1, source_target_pairs={{0,1},{1,0},{2,3},{3,2},{4,5},{5,4},{6,7},{7,6},{8,9},{9,8},{10,11... | collective-permute-start | bytes 258056 | tf_op jit(solution)/shard_map/ppermute | solution.py:443
  18.4 0.9 %collective-permute-start.1 = (bf16[24,1024]{1,0:T(8,128)(2,1)S(1)}, bf16[24,1024]{1,0:T(8,128)(2,1)S(1)}, u32[]{:S(2)}, u32[]{:S(2)}) collective-permute-start(bf16[24,1024]{1,0:T(8,128)(2,1)S(1)} %get-tuple-element.17.mine_ref.refs_8_), channel_id=1, source_target_pairs={{0,16},{16,0},{1,17},{17,1},{2,18},{18,2},{3,19},{19,3},{4,20},{20... | collective-permute-start | bytes 147464 | tf_op jit(solution)/shard_map/ppermute | solution.py:131
  19.3 3.1 %collective-permute-done.1.other_rest_ref = bf16[24,1024]{1,0:T(8,128)(2,1)S(1)} collective-permute-done((bf16[24,1024]{1,0:T(8,128)(2,1)S(1)}, bf16[24,1024]{1,0:T(8,128)(2,1)S(1)}, u32[]{:S(2)}, u32[]{:S(2)}) %collective-permute-start.1) | collective-permute-done | bytes 49184 | tf_op jit(solution)/shard_map/ppermute | solution.py:131
  22.5 0.1 shard_map.59.refs_0_
  22.6 0.1 collective-permute-start.2
  22.6 1.5 %collective-permute-start.3 = (bf16[96,1024]{1,0:T(8,128)(2,1)S(1)}, bf16[96,1024]{1,0:T(8,128)(2,1)S(1)}, u32[]{:S(2)}, u32[]{:S(2)}) collective-permute-start(bf16[96,1024]{1,0:T(8,128)(2,1)S(1)} %shard_map.59.refs_0_), channel_id=1, source_target_pairs={{0,8},{4,12},{8,0},{12,4},{1,9},{5,13},{9,1},{13,5},{2,10},{6,14},... | collective-permute-start | bytes 589832 | tf_op jit(solution)/shard_map/ppermute | solution.py:129
  24.1 0.4 collective-permute-start.4
  24.5 2.6 %collective-permute-start.13 = (f32[168,128]{1,0:T(8,128)S(1)}, f32[168,128]{1,0:T(8,128)S(1)}, u32[]{:S(2)}, u32[]{:S(2)}) collective-permute-start(f32[168,128]{1,0:T(8,128)S(1)} %get-tuple-element.26), channel_id=1, source_target_pairs={{0,2},{1,3},{2,0},{3,1},{4,6},{5,7},{6,4},{7,5},{8,10},{9,11},{10,... | collective-permute-start | bytes 258056 | tf_op jit(solution)/shard_map/ppermute | solution.py:443
  27.1 0.2 collective-permute-start.14
  27.3 6.5 %collective-permute-done.13.refs_2_ = f32[168,128]{1,0:T(8,128)S(1)} collective-permute-done((f32[168,128]{1,0:T(8,128)S(1)}, f32[168,128]{1,0:T(8,128)S(1)}, u32[]{:S(2)}, u32[]{:S(2)}) %collective-permute-start.13) | collective-permute-done | bytes 86048 | tf_op jit(solution)/shard_map/ppermute | solution.py:443
  33.8 3.5 %collective-permute-start.16 = (bf16[168,128]{1,0:T(8,128)(2,1)S(1)}, bf16[168,128]{1,0:T(8,128)(2,1)S(1)}, u32[]{:S(2)}, u32[]{:S(2)}) collective-permute-start(bf16[168,128]{1,0:T(8,128)(2,1)S(1)} %shard_map.62.refs_0_), channel_id=1, source_target_pairs={{0,2},{1,3},{2,0},{3,1},{4,6},{5,7},{6,4},{7,5},{8,10},{9,11},{10,... | collective-permute-start | bytes 129032 | tf_op jit(solution)/shard_map/ppermute | solution.py:458
  37.4 1.2 %collective-permute-start.17 = (bf16[168,128]{1,0:T(8,128)(2,1)S(1)}, bf16[168,128]{1,0:T(8,128)(2,1)S(1)}, u32[]{:S(2)}, u32[]{:S(2)}) collective-permute-start(bf16[168,128]{1,0:T(8,128)(2,1)S(1)} %shard_map.62.refs_0_), channel_id=1, source_target_pairs={{0,3},{1,2},{2,1},{3,0},{4,7},{5,6},{6,5},{7,4},{8,11},{9,10},{10,... | collective-permute-start | bytes 129032 | tf_op jit(solution)/shard_map/ppermute | solution.py:458
  38.6 1.2 %collective-permute-done.16.refs_0_ = bf16[168,128]{1,0:T(8,128)(2,1)S(1)} collective-permute-done((bf16[168,128]{1,0:T(8,128)(2,1)S(1)}, bf16[168,128]{1,0:T(8,128)(2,1)S(1)}, u32[]{:S(2)}, u32[]{:S(2)}) %collective-permute-start.16) | collective-permute-done | bytes 43040 | tf_op jit(solution)/shard_map/ppermute | solution.py:458
  39.8 1.3 %collective-permute-start.15 = (bf16[168,128]{1,0:T(8,128)(2,1)S(1)}, bf16[168,128]{1,0:T(8,128)(2,1)S(1)}, u32[]{:S(2)}, u32[]{:S(2)}) collective-permute-start(bf16[168,128]{1,0:T(8,128)(2,1)S(1)} %shard_map.62.refs_0_), channel_id=1, source_target_pairs={{0,1},{1,0},{2,3},{3,2},{4,5},{5,4},{6,7},{7,6},{8,9},{9,8},{10,11... | collective-permute-start | bytes 129032 | tf_op jit(solution)/shard_map/ppermute | solution.py:458
  41.2 2.5 %shard_map.60 = (bf16[3,432,192]{2,1,0:T(8,128)(2,1)S(1)}, bf16[27,48,192]{2,1,0:T(8,128)(2,1)S(1)}) custom-call(bf16[27,192,192]{2,1,0:T(8,128)(2,1)} %weight_ref.1), custom_call_target="tpu_custom_call" | custom-call | flops 95551488 | bytes 1990656 | tf_op jit(solution)/shard_map/pallas_call | solution.py:372
  43.7 0.1 collective-permute-done.17.refs_1_
  43.7 1.0 %collective-permute-start.19 = (bf16[336,128]{1,0:T(8,128)(2,1)S(1)}, bf16[336,128]{1,0:T(8,128)(2,1)S(1)}, u32[]{:S(2)}, u32[]{:S(2)}) collective-permute-start(bf16[336,128]{1,0:T(8,128)(2,1)S(1)} %shard_map.64.refs_9_), channel_id=1, source_target_pairs={{0,16},{16,0},{1,17},{17,1},{2,18},{18,2},{3,19},{19,3},{4,20},{20... | collective-permute-start | bytes 258056 | tf_op jit(solution)/shard_map/ppermute | solution.py:463
  44.7 1.2 %collective-permute-start.18 = (bf16[336,128]{1,0:T(8,128)(2,1)S(1)}, bf16[336,128]{1,0:T(8,128)(2,1)S(1)}, u32[]{:S(2)}, u32[]{:S(2)}) collective-permute-start(bf16[336,128]{1,0:T(8,128)(2,1)S(1)} %shard_map.63.refs_8_), channel_id=1, source_target_pairs={{0,16},{16,0},{1,17},{17,1},{2,18},{18,2},{3,19},{19,3},{4,20},{20... | collective-permute-start | bytes 258056 | tf_op jit(solution)/shard_map/ppermute | solution.py:463
  45.9 2.7 %shard_map.65 = (bf16[48,1024]{1,0:T(8,128)(2,1)}, bf16[48,1024]{1,0:T(8,128)(2,1)}, bf16[27,48,192]{2,1,0:T(8,128)(2,1)}) custom-call(bf16[96,1024]{1,0:T(8,128)(2,1)S(1)} %shard_map.59.refs_0_, bf16[96,1024]{1,0:T(8,128)(2,1)S(1)} %collective-permute-done.2.refs_1_, bf16[96,1024]{1,0:T(8,128)(2,1)S(1)} %collective-permute-done.3.refs_2_, ...), custom_call_target="tpu_custom_call" | custom-call | flops 1019215872 | bytes 2740224 | tf_op jit(solution)/shard_map/pallas_call | solution.py:372
  48.6 0.7 %collective-permute-done.18.near_ref = bf16[336,128]{1,0:T(8,128)(2,1)S(1)} collective-permute-done((bf16[336,128]{1,0:T(8,128)(2,1)S(1)}, bf16[336,128]{1,0:T(8,128)(2,1)S(1)}, u32[]{:S(2)}, u32[]{:S(2)}) %collective-permute-start.18) | collective-permute-done | bytes 86048 | tf_op jit(solution)/shard_map/ppermute | solution.py:463
  49.3 0.9 %shard_map.66 = bf16[27,48,192]{2,1,0:T(8,128)(2,1)} custom-call(bf16[27,48,192]{2,1,0:T(8,128)(2,1)} %get-tuple-element.30.half_out_ref, bf16[336,128]{1,0:T(8,128)(2,1)S(1)} %collective-permute-done.18.near_ref, bf16[336,128]{1,0:T(8,128)(2,1)S(1)} %collective-permute-done.19.far_ref), custom_call_target="tpu_custom_call", output_to_operand_aliasing={{}: (0, {})} | custom-call | bytes 669696 | tf_op jit(solution)/shard_map/pallas_call | solution.py:372
  (17 shorter events, 0.1 us)
Async XLA Ops:
  0.6 7.7 %collective-permute-start.10 = (bf16[48,1024]{1,0:T(8,128)(2,1)}, bf16[48,1024]{1,0:T(8,128)(2,1)S(1)}, u32[]{:S(2)}, u32[]{:S(2)}) collective-permute-start(bf16[48,1024]{1,0:T(8,128)(2,1)} %bitcast.7), channel_id=1, source_target_pairs={{0,24},{4,28},{8,16},{12,20},{16,8},{20,12},{24,0},{28,4},{1,25},{... | collective-permute-start | bytes 294920 | tf_op jit(solution)/shard_map/ppermute | solution.py:133
  4.6 5.4 %collective-permute-start.6 = (bf16[48,1024]{1,0:T(8,128)(2,1)}, bf16[48,1024]{1,0:T(8,128)(2,1)S(1)}, u32[]{:S(2)}, u32[]{:S(2)}) collective-permute-start(bf16[48,1024]{1,0:T(8,128)(2,1)} %bitcast.8), channel_id=1, source_target_pairs={{0,8},{4,12},{8,0},{12,4},{1,9},{5,13},{9,1},{13,5},{2,10},{6,14},... | collective-permute-start | bytes 294920 | tf_op jit(solution)/shard_map/ppermute | solution.py:129
  5.2 4.9 %collective-permute-start.8 = (bf16[48,1024]{1,0:T(8,128)(2,1)}, bf16[48,1024]{1,0:T(8,128)(2,1)S(1)}, u32[]{:S(2)}, u32[]{:S(2)}) collective-permute-start(bf16[48,1024]{1,0:T(8,128)(2,1)} %bitcast.9), channel_id=1, source_target_pairs={{0,16},{16,0},{1,17},{17,1},{2,18},{18,2},{3,19},{19,3},{4,20},{20... | collective-permute-start | bytes 294920 | tf_op jit(solution)/shard_map/ppermute | solution.py:131
  5.3 10.4 %collective-permute-start.5 = (bf16[48,1024]{1,0:T(8,128)(2,1)}, bf16[48,1024]{1,0:T(8,128)(2,1)S(1)}, u32[]{:S(2)}, u32[]{:S(2)}) collective-permute-start(bf16[48,1024]{1,0:T(8,128)(2,1)} %bitcast.10), channel_id=1, source_target_pairs={{0,4},{4,0},{8,12},{12,8},{1,5},{5,1},{9,13},{13,9},{2,6},{6,2},{1... | collective-permute-start | bytes 294920 | tf_op jit(solution)/shard_map/ppermute | solution.py:129
  8.3 7.3 %collective-permute-start.11 = (bf16[48,1024]{1,0:T(8,128)(2,1)S(1)}, bf16[48,1024]{1,0:T(8,128)(2,1)S(1)}, u32[]{:S(2)}, u32[]{:S(2)}) collective-permute-start(bf16[48,1024]{1,0:T(8,128)(2,1)S(1)} %collective-permute-done.10.refs_6_), channel_id=1, source_target_pairs={{0,4},{4,0},{8,12},{12,8},{1,5},{5,1},{9,13},{13,9},{2,6},{6,2},{1... | collective-permute-start | bytes 294920 | tf_op jit(solution)/shard_map/ppermute | solution.py:129
  10.1 5.6 %collective-permute-start.7 = (bf16[48,1024]{1,0:T(8,128)(2,1)S(1)}, bf16[48,1024]{1,0:T(8,128)(2,1)S(1)}, u32[]{:S(2)}, u32[]{:S(2)}) collective-permute-start(bf16[48,1024]{1,0:T(8,128)(2,1)S(1)} %collective-permute-done.6.refs_2_), channel_id=1, source_target_pairs={{0,4},{4,0},{8,12},{12,8},{1,5},{5,1},{9,13},{13,9},{2,6},{6,2},{1... | collective-permute-start | bytes 294920 | tf_op jit(solution)/shard_map/ppermute | solution.py:129
  10.1 5.6 %collective-permute-start.9 = (bf16[48,1024]{1,0:T(8,128)(2,1)S(1)}, bf16[48,1024]{1,0:T(8,128)(2,1)S(1)}, u32[]{:S(2)}, u32[]{:S(2)}) collective-permute-start(bf16[48,1024]{1,0:T(8,128)(2,1)S(1)} %collective-permute-done.8.refs_4_), channel_id=1, source_target_pairs={{0,4},{4,0},{8,12},{12,8},{1,5},{5,1},{9,13},{13,9},{2,6},{6,2},{1... | collective-permute-start | bytes 294920 | tf_op jit(solution)/shard_map/ppermute | solution.py:129
  11.5 4.2 %collective-permute-start = (bf16[24,1024]{1,0:T(8,128)(2,1)S(1)}, bf16[24,1024]{1,0:T(8,128)(2,1)S(1)}, u32[]{:S(2)}, u32[]{:S(2)}) collective-permute-start(bf16[24,1024]{1,0:T(8,128)(2,1)S(1)} %get-tuple-element.18.sent_ref), channel_id=1, source_target_pairs={{0,16},{16,0},{1,17},{17,1},{2,18},{18,2},{3,19},{19,3},{4,20},{20... | collective-permute-start | bytes 147464 | tf_op jit(solution)/shard_map/ppermute | solution.py:131
  16.8 10.3 %collective-permute-start.12 = (f32[168,128]{1,0:T(8,128)S(1)}, f32[168,128]{1,0:T(8,128)S(1)}, u32[]{:S(2)}, u32[]{:S(2)}) collective-permute-start(f32[168,128]{1,0:T(8,128)S(1)} %get-tuple-element.25), channel_id=1, source_target_pairs={{0,1},{1,0},{2,3},{3,2},{4,5},{5,4},{6,7},{7,6},{8,9},{9,8},{10,11... | collective-permute-start | bytes 258056 | tf_op jit(solution)/shard_map/ppermute | solution.py:443
  18.4 4.1 %collective-permute-start.1 = (bf16[24,1024]{1,0:T(8,128)(2,1)S(1)}, bf16[24,1024]{1,0:T(8,128)(2,1)S(1)}, u32[]{:S(2)}, u32[]{:S(2)}) collective-permute-start(bf16[24,1024]{1,0:T(8,128)(2,1)S(1)} %get-tuple-element.17.mine_ref.refs_8_), channel_id=1, source_target_pairs={{0,16},{16,0},{1,17},{17,1},{2,18},{18,2},{3,19},{19,3},{4,20},{20... | collective-permute-start | bytes 147464 | tf_op jit(solution)/shard_map/ppermute | solution.py:131
  22.6 23.4 %collective-permute-start.2 = (bf16[96,1024]{1,0:T(8,128)(2,1)S(1)}, bf16[96,1024]{1,0:T(8,128)(2,1)S(1)}, u32[]{:S(2)}, u32[]{:S(2)}) collective-permute-start(bf16[96,1024]{1,0:T(8,128)(2,1)S(1)} %shard_map.59.refs_0_), channel_id=1, source_target_pairs={{0,4},{4,0},{8,12},{12,8},{1,5},{5,1},{9,13},{13,9},{2,6},{6,2},{1... | collective-permute-start | bytes 589832 | tf_op jit(solution)/shard_map/ppermute | solution.py:129
  22.6 23.3 %collective-permute-start.3 = (bf16[96,1024]{1,0:T(8,128)(2,1)S(1)}, bf16[96,1024]{1,0:T(8,128)(2,1)S(1)}, u32[]{:S(2)}, u32[]{:S(2)}) collective-permute-start(bf16[96,1024]{1,0:T(8,128)(2,1)S(1)} %shard_map.59.refs_0_), channel_id=1, source_target_pairs={{0,8},{4,12},{8,0},{12,4},{1,9},{5,13},{9,1},{13,5},{2,10},{6,14},... | collective-permute-start | bytes 589832 | tf_op jit(solution)/shard_map/ppermute | solution.py:129
  24.1 21.8 %collective-permute-start.4 = (bf16[96,1024]{1,0:T(8,128)(2,1)S(1)}, bf16[96,1024]{1,0:T(8,128)(2,1)S(1)}, u32[]{:S(2)}, u32[]{:S(2)}) collective-permute-start(bf16[96,1024]{1,0:T(8,128)(2,1)S(1)} %shard_map.59.refs_0_), channel_id=1, source_target_pairs={{0,12},{4,8},{8,4},{12,0},{1,13},{5,9},{9,5},{13,1},{2,14},{6,10},... | collective-permute-start | bytes 589832 | tf_op jit(solution)/shard_map/ppermute | solution.py:129
  24.5 9.3 %collective-permute-start.13 = (f32[168,128]{1,0:T(8,128)S(1)}, f32[168,128]{1,0:T(8,128)S(1)}, u32[]{:S(2)}, u32[]{:S(2)}) collective-permute-start(f32[168,128]{1,0:T(8,128)S(1)} %get-tuple-element.26), channel_id=1, source_target_pairs={{0,2},{1,3},{2,0},{3,1},{4,6},{5,7},{6,4},{7,5},{8,10},{9,11},{10,... | collective-permute-start | bytes 258056 | tf_op jit(solution)/shard_map/ppermute | solution.py:443
  27.1 6.7 %collective-permute-start.14 = (f32[168,128]{1,0:T(8,128)S(1)}, f32[168,128]{1,0:T(8,128)S(1)}, u32[]{:S(2)}, u32[]{:S(2)}) collective-permute-start(f32[168,128]{1,0:T(8,128)S(1)} %get-tuple-element.27), channel_id=1, source_target_pairs={{0,3},{1,2},{2,1},{3,0},{4,7},{5,6},{6,5},{7,4},{8,11},{9,10},{10,... | collective-permute-start | bytes 258056 | tf_op jit(solution)/shard_map/ppermute | solution.py:443
  33.8 6.0 %collective-permute-start.16 = (bf16[168,128]{1,0:T(8,128)(2,1)S(1)}, bf16[168,128]{1,0:T(8,128)(2,1)S(1)}, u32[]{:S(2)}, u32[]{:S(2)}) collective-permute-start(bf16[168,128]{1,0:T(8,128)(2,1)S(1)} %shard_map.62.refs_0_), channel_id=1, source_target_pairs={{0,2},{1,3},{2,0},{3,1},{4,6},{5,7},{6,4},{7,5},{8,10},{9,11},{10,... | collective-permute-start | bytes 129032 | tf_op jit(solution)/shard_map/ppermute | solution.py:458
  37.4 6.3 %collective-permute-start.17 = (bf16[168,128]{1,0:T(8,128)(2,1)S(1)}, bf16[168,128]{1,0:T(8,128)(2,1)S(1)}, u32[]{:S(2)}, u32[]{:S(2)}) collective-permute-start(bf16[168,128]{1,0:T(8,128)(2,1)S(1)} %shard_map.62.refs_0_), channel_id=1, source_target_pairs={{0,3},{1,2},{2,1},{3,0},{4,7},{5,6},{6,5},{7,4},{8,11},{9,10},{10,... | collective-permute-start | bytes 129032 | tf_op jit(solution)/shard_map/ppermute | solution.py:458
  39.8 4.9 %collective-permute-start.15 = (bf16[168,128]{1,0:T(8,128)(2,1)S(1)}, bf16[168,128]{1,0:T(8,128)(2,1)S(1)}, u32[]{:S(2)}, u32[]{:S(2)}) collective-permute-start(bf16[168,128]{1,0:T(8,128)(2,1)S(1)} %shard_map.62.refs_0_), channel_id=1, source_target_pairs={{0,1},{1,0},{2,3},{3,2},{4,5},{5,4},{6,7},{7,6},{8,9},{9,8},{10,11... | collective-permute-start | bytes 129032 | tf_op jit(solution)/shard_map/ppermute | solution.py:458
  43.7 4.9 %collective-permute-start.19 = (bf16[336,128]{1,0:T(8,128)(2,1)S(1)}, bf16[336,128]{1,0:T(8,128)(2,1)S(1)}, u32[]{:S(2)}, u32[]{:S(2)}) collective-permute-start(bf16[336,128]{1,0:T(8,128)(2,1)S(1)} %shard_map.64.refs_9_), channel_id=1, source_target_pairs={{0,16},{16,0},{1,17},{17,1},{2,18},{18,2},{3,19},{19,3},{4,20},{20... | collective-permute-start | bytes 258056 | tf_op jit(solution)/shard_map/ppermute | solution.py:463
  44.7 4.6 %collective-permute-start.18 = (bf16[336,128]{1,0:T(8,128)(2,1)S(1)}, bf16[336,128]{1,0:T(8,128)(2,1)S(1)}, u32[]{:S(2)}, u32[]{:S(2)}) collective-permute-start(bf16[336,128]{1,0:T(8,128)(2,1)S(1)} %shard_map.63.refs_8_), channel_id=1, source_target_pairs={{0,16},{16,0},{1,17},{17,1},{2,18},{18,2},{3,19},{19,3},{4,20},{20... | collective-permute-start | bytes 258056 | tf_op jit(solution)/shard_map/ppermute | solution.py:463
